TPU v7x, 32 devices: a whole 2x2x4 slice. The times are simulated.
32 devices in a mesh: grp: 2 (over y), row: 4 (over z), col: 2 (over x), rep: 2 (over core).
Axes of the slice: x: 2, y: 2, z: 4, core: 2. Of those that a mesh axis runs over, the one named last changes fastest.
Arguments:
- emb_row: bfloat16 [2048, 1280], P(('grp', 'row', 'rep'), 'col'), parts along dimension 0, may hold values from -6 to 6
- emb_col: bfloat16 [512, 1280], P(('grp', 'col'), 'row'), parts along dimension 0, may hold values from -6 to 6
- proj_row: bfloat16 [1280, 64], replicated, may hold values from -0.15625 to 0.15625
- proj_col: bfloat16 [1280, 64], replicated, may hold values from -0.15625 to 0.15625
- pair_out: bfloat16 [64, 64], replicated, may hold values from -0.75 to 0.75
- pair_bias: float32 [64], replicated, may hold values from -3 to 3
- conv_weight: bfloat16 [3, 3, 64, 64], replicated, may hold values from -0.25 to 0.25
- conv_bias: float32 [64], replicated, may hold values from -3 to 3
- target: bfloat16 [64, 2048, 256], P(None, ('grp', 'row', 'rep'), 'col'), parts along dimension 1, may hold values from -6 to 6
- kept_tiles: int32 [16, 2], P(('grp', 'row', 'rep'), 'col'), parts along dimension 0, may hold values 0 or 1
Outputs:
- cell_loss: float32 [2048, 256], P(('grp', 'row', 'rep'), 'col'), parts along dimension 0
- grad_conv: float32 [6, 3, 64, 64], P('grp'), parts along dimension 0
- grad_bias: float32 [128], P('grp'), parts along dimension 0
There are 2 independent parts, one for each index of `grp`. A program takes and returns all parts, laid end to end along the dimension named above; an argument that names none is the same for every part. Nothing has to cross between parts.
All inputs are finite; a program needn't handle non-finite values. No bound on the sum of `kept_tiles` on one device may be relied on, other than what follows from the above.
Results may differ from a plain program's by a relative error of at most 0.0025.
Values may be sent and summed in bfloat16 or wider, within the bound.
A program may use at most 128 MiB of HBM per device.

v0:
```python
import functools

import jax
import jax.numpy as jnp
from jax import lax
from jax.experimental import pallas as pl
from jax.experimental.pallas import tpu as pltpu
from jax.sharding import PartitionSpec as P

MESH = pl.DeviceIdType.MESH
F32 = jnp.float32
BF16 = jnp.bfloat16
NT = (((1,), (1,)), ((), ()))


def loop(low, high, body):
    if high - low <= 16:
        for d in range(low, high):
            body(d)
    else:
        lax.fori_loop(low, high, lambda d, _: (body(d), 0)[1], 0)


def columns(ref, width, index, count):
    everything = ref.shape[1]
    if width % 128 == 0:
        return ref[:, pl.ds(pl.multiple_of(index * width, 128), width)]
    offset = max(i * width % 128 for i in range(count))
    window = min(-(-(offset + width) // 128) * 128, everything)
    tile = index * width // 128
    if any(i * width // 128 * 128 + window > everything for i in range(count)):
        tile = jnp.minimum(tile, (everything - window) // 128)
    value = ref[:, pl.ds(pl.multiple_of(tile * 128, 128), window)].astype(F32)
    shift = window - (index * width - tile * 128)
    return pltpu.roll(value, shift % window, 1)[:, 0:width].astype(BF16)


def kernel(
    sizes,
    emb_row_hbm,
    emb_col_hbm,
    proj_row_hbm,
    proj_col_hbm,
    pair_out,
    pair_bias,
    conv_weight_hbm,
    conv_bias,
    target,
    kept,
    loss_out,
    full,
    emb_row,
    emb_col,
    proj_row,
    proj_col,
    conv_weight,
    in_sem,
    rowtail,
    coltail,
    rowbuf,
    rowedge,
    colbuf,
    coledge,
    row_feat,
    col_wide,
    wide_t,
    target_in,
    target32,
    hid,
    base,
    grad_in,
    weight_f,
    total,
    bias_acc,
    part,
    reduced,
    target_sem,
    row_send,
    row_recv,
    redge_send,
    redge_recv,
    col_send,
    col_recv,
    cedge_send,
    cedge_recv,
    rs_send,
    rs_recv,
    ag_send,
    ag_recv,
):
    n_row, n_col, n_rep, edge, chan, chunk = sizes
    n_all = n_row * n_col * n_rep
    pairs = edge // 2
    row, col, rep = lax.axis_index("row"), lax.axis_index("col"), lax.axis_index("rep")
    line = row * n_rep + rep
    n_line = n_row * n_rep
    me = line * n_col + col

    def device(index):
        across = index % n_col
        along = index // n_col
        return {"row": along // n_rep, "rep": along % n_rep, "col": across}

    barrier = pltpu.get_barrier_semaphore()
    loop(
        1,
        n_all,
        lambda d: pl.semaphore_signal(
            barrier, inc=1, device_id=device((me + d) % n_all), device_id_type=MESH
        ),
    )

    inputs = [
        pltpu.make_async_copy(src, dst, in_sem.at[i])
        for i, (src, dst) in enumerate(
            (
                (emb_row_hbm, emb_row),
                (proj_row_hbm, proj_row),
                (emb_col_hbm, emb_col),
                (proj_col_hbm, proj_col),
                (conv_weight_hbm, conv_weight),
            )
        )
    ]
    for copy in inputs:
        copy.start()
    fetch = pltpu.make_async_copy(target, target_in, target_sem)
    fetch.start()

    def rounded(x):
        return x.astype(BF16).astype(F32)

    keep = kept[0, 0].astype(F32)
    for copy in inputs[2:4]:
        copy.wait()
    part_col = jnp.dot(
        columns(proj_col, emb_col.shape[0], row, n_row),
        emb_col[...],
        preferred_element_type=F32,
    )
    for copy in inputs[0:2]:
        copy.wait()
    part_row = lax.dot_general(
        columns(proj_row, emb_row.shape[1], col, n_col),
        emb_row[...],
        NT,
        preferred_element_type=F32,
    )
    rank = part_row.shape[0]
    colbuf[row] = part_col.astype(BF16)
    rowbuf[col, 0:rank, :] = part_row.astype(BF16)
    rowbuf[col, rank:, :] = jnp.full((16, edge), keep, F32).astype(BF16)
    turned = rounded(part_col).T
    coltail[0] = turned[edge - 8 :]
    coltail[1] = turned[0:8]
    turned = rounded(part_row).T
    rowtail[0, 0:8] = turned[edge - 8 :]
    rowtail[1, 0:8] = turned[0:8]
    for side in range(2):
        rowtail[side, 8:16] = jnp.full((8, rank), keep, F32)

    pl.semaphore_wait(barrier, n_all - 1)

    def row_copy(d, src):
        return pltpu.make_async_remote_copy(
            src_ref=rowbuf.at[src],
            dst_ref=rowbuf.at[src],
            send_sem=row_send.at[d],
            recv_sem=row_recv.at[src],
            device_id={"col": (col + d) % n_col},
            device_id_type=MESH,
        )

    def redge_copy(side, d, src):
        to = (line + (1 if side == 0 else n_line - 1)) % n_line
        return pltpu.make_async_remote_copy(
            src_ref=rowtail.at[side],
            dst_ref=rowedge.at[side, src],
            send_sem=redge_send.at[side, d],
            recv_sem=redge_recv.at[side, src],
            device_id={"row": to // n_rep, "rep": to % n_rep, "col": (col + d) % n_col},
            device_id_type=MESH,
        )

    def col_copy(d, src):
        return pltpu.make_async_remote_copy(
            src_ref=colbuf.at[src],
            dst_ref=colbuf.at[src],
            send_sem=col_send.at[d],
            recv_sem=col_recv.at[src],
            device_id={"row": (row + d) % n_row},
            device_id_type=MESH,
        )

    def cedge_copy(side, d, src):
        to = (col + (1 if side == 0 else n_col - 1)) % n_col
        return pltpu.make_async_remote_copy(
            src_ref=coltail.at[side],
            dst_ref=coledge.at[side, src],
            send_sem=cedge_send.at[side, d],
            recv_sem=cedge_recv.at[side, src],
            device_id={"row": (row + d) % n_row, "col": to},
            device_id_type=MESH,
        )

    loop(1, n_row, lambda d: col_copy(d, row).start())
    loop(1, n_col, lambda d: row_copy(d, col).start())
    for side in range(2):
        loop(0, n_row, lambda d: cedge_copy(side, d, row).start())
        loop(0, n_col, lambda d: redge_copy(side, d, col).start())

    fetch.wait()
    inputs[4].wait()

    def widen(c, _):
        start = pl.multiple_of(c * edge, edge)
        target32[pl.ds(start, edge), :] = target_in[c].astype(F32)
        return 0

    lax.fori_loop(0, chan, widen, 0, unroll=4)
    for a in range(3):
        for b in range(3):
            weight_f[b * chan : (b + 1) * chan, a * chan : (a + 1) * chan] = conv_weight[
                a, b
            ].astype(F32)
    weight_t = weight_f[...].T.astype(BF16)
    out_t = pair_out[...].astype(F32).T
    pair_b = jnp.broadcast_to(pair_bias[...], (128, chan)).T
    conv_b = jnp.broadcast_to(conv_bias[...], (128, chan)).T
    zeros = jnp.zeros((2 * chan, 2 * edge), BF16)
    grad_in[0 : 2 * chan, :] = zeros
    grad_in[(pairs + 2) * chan : (pairs + 4) * chan, :] = zeros
    base[0 : 2 * chan, :] = zeros.astype(F32)
    base[(pairs + 2) * chan : (pairs + 4) * chan, :] = zeros.astype(F32)
    bias_acc[...] = jnp.zeros_like(bias_acc)
    total[...] = jnp.zeros_like(total)

    loop(1, n_row, lambda d: col_copy(d, (row + n_row - d) % n_row).wait_recv())
    loop(1, n_col, lambda d: row_copy(d, (col + n_col - d) % n_col).wait_recv())
    for side in range(2):
        loop(0, n_row, lambda d: cedge_copy(side, d, (row + n_row - d) % n_row).wait_recv())
        loop(0, n_col, lambda d: redge_copy(side, d, (col + n_col - d) % n_col).wait_recv())

    def summed(terms):
        return sum(x.astype(F32) for x in terms)

    row_feat[0:8, :] = rounded(summed(rowedge[0, c, 0:8, :] for c in range(n_col)))
    row_feat[8 : edge + 8, :] = rounded(summed(rowbuf[c, 0:rank, :] for c in range(n_col))).T
    row_feat[edge + 8 :, :] = rounded(summed(rowedge[1, c, 0:8, :] for c in range(n_col)))
    col_wide[0:8, :] = summed(coledge[0, r] for r in range(n_row))
    col_wide[8 : edge + 8, :] = summed(colbuf[r] for r in range(n_row)).T
    col_wide[edge + 8 :, :] = summed(coledge[1, r] for r in range(n_row))
    for b in range(3):
        wide_t[b * edge : (b + 1) * edge, :] = col_wide[
            6 + 2 * b : 6 + 2 * b + edge, :
        ].astype(BF16)

    lane = lax.broadcasted_iota(jnp.int32, (1, edge), 1)
    before, after = (col + n_col - 1) % n_col, (col + 1) % n_col
    has_before = (col > 0).astype(F32)
    has_after = (col < n_col - 1).astype(F32)

    def masks(get, valid):
        here, left, right = (
            jnp.broadcast_to(get(c), (1, edge)) * scale
            for c, scale in ((col, valid), (before, valid * has_before), (after, valid * has_after))
        )
        return (jnp.where(lane < 2, left, here), here, jnp.where(lane >= edge - 2, right, here))

    top = masks(lambda c: rowedge[0, c, 8:9, 0:1], (line > 0).astype(F32))
    middle = masks(lambda c: rowbuf[c, rank:, 0:1].astype(F32)[0:1], jnp.float32(1))
    bottom = masks(lambda c: rowedge[1, c, 8:9, 0:1], (line < n_line - 1).astype(F32))

    def features(pair, count, mask, inner):
        scaled = []
        for r in range(2 * count):
            feat = row_feat[pl.ds(2 * pair + 8 + r, 1), :]
            scaled.append((out_t * feat).astype(BF16))
        product = lax.dot_general(
            jnp.concatenate(scaled, axis=0), wide_t[...], NT, preferred_element_type=F32
        )
        for r in range(2 * count):
            p = pair + r // 2
            lanes = slice((r % 2) * edge, (r % 2 + 1) * edge)
            for b in range(3):
                value = product[r * chan : (r + 1) * chan, b * edge : (b + 1) * edge] + pair_b
                start = pl.multiple_of((p + 1) * 3 * chan + b * chan, chan)
                hid[pl.ds(start, chan), lanes] = (jnp.maximum(value, 0.0) * mask[b]).astype(BF16)
                if inner and b == 1:
                    aim = target32[pl.ds(2 * pair + r, chan, stride=edge), :]
                    start = pl.multiple_of((p + 2) * chan, chan)
                    base[pl.ds(start, chan), lanes] = (value + conv_b) - aim

    features(-1, 1, top, False)
    features(pairs, 1, bottom, False)
    group = 4

    def conv_of(p):
        start = pl.multiple_of((p + 1) * 3 * chan, 3 * chan)
        return jnp.dot(weight_t, hid[pl.ds(start, 3 * chan), :], preferred_element_type=F32)

    def slot(p):
        return pl.ds(pl.multiple_of((p + 2) * chan, chan), chan)

    def spread(p, done):
        y = conv_of(p)
        base[slot(p + 1), :] += y[0:chan]
        base[slot(p), :] += y[chan : 2 * chan]
        if done:
            differ = (base[slot(p - 1), :] + y[2 * chan :]) * keep
            grad_in[slot(p - 1), :] = differ.astype(BF16)
            bias_acc[...] += differ
            loss = 0.5 * jnp.sum(differ * differ, axis=0, keepdims=True)
            loss_out[pl.ds(2 * (p - 1), 1), :] = loss[:, 0:edge]
            loss_out[pl.ds(2 * (p - 1) + 1, 1), :] = loss[:, edge : 2 * edge]

    def grads(first, count):
        value = total[...]
        for r in range(count):
            p = first + r
            start = pl.multiple_of((p + 1) * 3 * chan, 3 * chan)
            near = pl.multiple_of((p + 1) * chan, chan)
            value = value + lax.dot_general(
                hid[pl.ds(start, 3 * chan), :],
                grad_in[pl.ds(near, 3 * chan), :],
                NT,
                preferred_element_type=F32,
            )
        total[...] = value

    for g in range(3):
        features(g * group, group, middle, True)
    spread(-1, False)
    spread(0, False)
    for r in range(group):
        spread(1 + r, True)
    lag = 2 * group - 1

    def step(g, _):
        grads(g * group - 3 * group - 1, group)
        for r in range(group):
            spread(g * group - lag + r, True)
        features(g * group, group, middle, True)
        return 0

    lax.fori_loop(3, pairs // group, step, 0)

    def conv_step(g, _):
        for r in range(group):
            spread(pairs - lag + g * group + r, True)
        return 0

    lax.fori_loop(0, 2, conv_step, 0)

    def grad_step(g, _):
        grads(pairs - 3 * group - 1 + g * 7, 7)
        return 0

    lax.fori_loop(0, 2, grad_step, 0)

    norm = 1.0 / (edge * edge)
    half = 3 * chan // 2
    rows = 3 * chan + half
    sums = total[...] * norm
    flat = jnp.concatenate(
        [
            sums[:, 0 : 2 * chan],
            jnp.concatenate([sums[0:half, 2 * chan :], sums[half:, 2 * chan :]], axis=1),
        ],
        axis=0,
    )
    bias_sum = lax.dot_general(
        jnp.ones((8, 2 * edge), F32),
        bias_acc[...] * norm,
        NT,
        precision=lax.Precision.HIGHEST,
        preferred_element_type=F32,
    )
    part[0:rows, :] = flat
    part[rows : rows + 8, :] = jnp.concatenate([bias_sum, bias_sum], axis=1)
    rest = n_all * chunk - rows - 8
    if rest > 0:
        part[rows + 8 :, :] = jnp.zeros((rest, 128), F32)

    def piece(index):
        return pl.ds(pl.multiple_of(index * chunk, 8), chunk)

    def rs_copy(d, to, src):
        return pltpu.make_async_remote_copy(
            src_ref=part.at[piece(to)],
            dst_ref=reduced.at[src],
            send_sem=rs_send.at[d],
            recv_sem=rs_recv.at[src],
            device_id=device(to),
            device_id_type=MESH,
        )

    def ag_copy(d, to, src):
        return pltpu.make_async_remote_copy(
            src_ref=full.at[src],
            dst_ref=full.at[src],
            send_sem=ag_send.at[d],
            recv_sem=ag_recv.at[src],
            device_id=device(to),
            device_id_type=MESH,
        )

    loop(1, n_all, lambda d: rs_copy(d, (me + d) % n_all, me).start())
    reduced[me] = part[piece(me), :]
    loop(1, n_all, lambda d: rs_copy(d, (me + d) % n_all, (me + n_all - d) % n_all).wait_recv())
    if n_all <= 16:
        own = sum(reduced[r] for r in range(n_all))
    else:
        own = lax.fori_loop(
            0, n_all, lambda r, x: x + reduced[r], jnp.zeros((chunk, 128), F32)
        )
    full[me] = own
    loop(1, n_all, lambda d: ag_copy(d, (me + d) % n_all, me).start())
    loop(1, n_all, lambda d: ag_copy(d, (me + d) % n_all, (me + n_all - d) % n_all).wait_recv())

    loop(1, n_row, lambda d: col_copy(d, row).wait_send())
    loop(1, n_col, lambda d: row_copy(d, col).wait_send())
    for side in range(2):
        loop(0, n_row, lambda d: cedge_copy(side, d, row).wait_send())
        loop(0, n_col, lambda d: redge_copy(side, d, col).wait_send())
    loop(1, n_all, lambda d: rs_copy(d, (me + d) % n_all, me).wait_send())
    loop(1, n_all, lambda d: ag_copy(d, (me + d) % n_all, me).wait_send())


def finish(loss_in, gathered, loss_out, conv_grad_out, bias_out, full):
    n_all, chunk = gathered.shape[0:2]

    def place(r):
        full[pl.ds(r * chunk, chunk), :] = gathered[r]

    loop(0, n_all, place)
    chan = bias_out.shape[1]
    half = 3 * chan // 2
    rows = 3 * chan + half
    loss_out[...] = loss_in[...]
    for b in range(3):
        low = b * chan
        conv_grad_out[2, b] = full[low : low + chan, 0:chan]
        conv_grad_out[1, b] = full[low : low + chan, chan : 2 * chan]
    low = 3 * chan
    conv_grad_out[0, 0] = full[low : low + chan, 0:chan]
    conv_grad_out[0, 1, 0 : half - chan] = full[low + chan : low + half, 0:chan]
    conv_grad_out[0, 1, half - chan :] = full[low : low + 2 * chan - half, chan : 2 * chan]
    conv_grad_out[0, 2] = full[low + 2 * chan - half : low + half, chan : 2 * chan]
    bias_out[...] = full[rows : rows + 1, 0:chan]


def solution(mesh):
    n_row, n_col, n_rep = (mesh.shape[axis] for axis in ("row", "col", "rep"))
    n_all = n_row * n_col * n_rep

    def per_device(
        emb_row,
        emb_col,
        proj_row,
        proj_col,
        pair_out,
        pair_bias,
        conv_weight,
        conv_bias,
        target,
        kept_tiles,
    ):
        chan, edge = target.shape[0], target.shape[1]
        rank = pair_out.shape[0]
        pairs = edge // 2
        used = 3 * chan + 3 * chan // 2 + 8
        chunk = 8 * pl.cdiv(used, 8 * n_all)

        dma = pltpu.SemaphoreType.DMA
        vmem = pl.BlockSpec(memory_space=pltpu.VMEM)
        hbm = pl.BlockSpec(memory_space=pl.ANY)
        loss, sums = pl.pallas_call(
            functools.partial(kernel, (n_row, n_col, n_rep, edge, chan, chunk)),
            out_shape=(
                jax.ShapeDtypeStruct((edge, edge), F32),
                jax.ShapeDtypeStruct((n_all, chunk, 128), F32),
            ),
            in_specs=[hbm] * 4
            + [vmem] * 2
            + [hbm, vmem, hbm, pl.BlockSpec(memory_space=pltpu.SMEM)],
            out_specs=(vmem,) * 2,
            scratch_shapes=[
                pltpu.VMEM(emb_row.shape, BF16),
                pltpu.VMEM(emb_col.shape[::-1], BF16),
                pltpu.VMEM(proj_row.shape[::-1], BF16),
                pltpu.VMEM(proj_col.shape[::-1], BF16),
                pltpu.VMEM(conv_weight.shape, BF16),
                dma((5,)),
                pltpu.VMEM((2, 16, rank), F32),
                pltpu.VMEM((2, 8, rank), F32),
                pltpu.VMEM((n_col, rank + 16, edge), BF16),
                pltpu.VMEM((2, n_col, 16, rank), F32),
                pltpu.VMEM((n_row, rank, edge), BF16),
                pltpu.VMEM((2, n_row, 8, rank), F32),
                pltpu.VMEM((edge + 16, rank), F32),
                pltpu.VMEM((edge + 16, rank), F32),
                pltpu.VMEM((3 * edge, rank), BF16),
                pltpu.VMEM((chan, edge, edge), BF16),
                pltpu.VMEM((chan * edge, edge), F32),
                pltpu.VMEM(((pairs + 2) * 3 * chan, 2 * edge), BF16),
                pltpu.VMEM(((pairs + 4) * chan, 2 * edge), F32),
                pltpu.VMEM(((pairs + 4) * chan, 2 * edge), BF16),
                pltpu.VMEM((3 * chan, 3 * chan), F32),
                pltpu.VMEM((3 * chan, 3 * chan), F32),
                pltpu.VMEM((chan, 2 * edge), F32),
                pltpu.VMEM((n_all * chunk, 128), F32),
                pltpu.VMEM((n_all, chunk, 128), F32),
                pltpu.SemaphoreType.DMA,
                dma((n_col,)),
                dma((n_col,)),
                dma((2, n_col)),
                dma((2, n_col)),
                dma((n_row,)),
                dma((n_row,)),
                dma((2, n_row)),
                dma((2, n_row)),
                dma((n_all,)),
                dma((n_all,)),
                dma((n_all,)),
                dma((n_all,)),
            ],
            compiler_params=pltpu.CompilerParams(collective_id=0, has_side_effects=True),
            name="pair_step",
        )(
            emb_row,
            emb_col.T,
            proj_row.T,
            proj_col.T,
            pair_out,
            pair_bias.reshape(1, chan),
            conv_weight,
            conv_bias.reshape(1, chan),
            target,
            kept_tiles,
        )
        loss, grads, bias = pl.pallas_call(
            finish,
            out_shape=(
                jax.ShapeDtypeStruct((edge, edge), F32),
                jax.ShapeDtypeStruct((3, 3, chan, chan), F32),
                jax.ShapeDtypeStruct((1, chan), F32),
            ),
            in_specs=[vmem] * 2,
            out_specs=(vmem,) * 3,
            scratch_shapes=[pltpu.VMEM((n_all * chunk, 128), F32)],
            name="finish",
        )(loss, sums)
        return loss, grads, bias.reshape(chan)

    in_specs = (
        P(("grp", "row", "rep"), "col"),
        P(("grp", "col"), "row"),
        P(),
        P(),
        P(),
        P(),
        P(),
        P(),
        P(None, ("grp", "row", "rep"), "col"),
        P(("grp", "row", "rep"), "col"),
    )
    out_specs = (P(("grp", "row", "rep"), "col"), P("grp", None, None, None), P("grp"))
    return jax.shard_map(
        per_device, mesh=mesh, in_specs=in_specs, out_specs=out_specs, check_vma=False
    )
```

profile of v0, /device:TPU:1, one launch (start us, length us, event | category | flops | bytes accessed | tf_op | source)
XLA Modules:
  0.0 39.4 jit_solution(3815731676029167618)
XLA Ops:
  1.3 36.4 %pair_step.1 = (f32[128,128]{1,0:T(8,128)}, f32[16,24,128]{2,1,0:T(8,128)}) custom-call(bf16[128,640]{1,0:T(8,128)(2,1)} %emb_row_hbm.1, bf16[320,128]{1,0:T(8,128)(2,1)} %bitcast.8, bf16[64,1280]{1,0:T(8,128)(2,1)} %bitcast.6, bf16[64,1280]{1,0:T(8,128)(2,1)} %bitcast.7, bf16[64,64]{1,0:T(8,128)(2,1)} %pair_out.1, f32[1,64]{1,0:T(1,128)} %bitcast.9, ...), custom_call_target="tpu_custom_call" | custom-call | tf_op jit(solution)/shard_map/pair_step/pallas_call | solution.py:478
  37.7 1.8 %finish.1 = (f32[128,128]{1,0:T(8,128)}, f32[3,3,64,64]{3,2,1,0:T(8,128)}, f32[1,64]{1,0:T(1,128)}) custom-call(f32[128,128]{1,0:T(8,128)} %get-tuple-element.8.loss_in, f32[16,24,128]{2,1,0:T(8,128)} %get-tuple-element.9.gathered), custom_call_target="tpu_custom_call" | custom-call | tf_op jit(solution)/shard_map/finish/pallas_call | solution.py:542
where the time goes:
time: 39.7 us; the launch traced here: 39.4 us
  Pallas kernels  38.2 us (96%)
  between operations  1.29 us (3%)
    pallas_call x1, Pallas kernels, per_device(): pl.pallas_call(functools.partial(kernel, (n_row, n_col, n_rep, edge, chan...  36.4 us
    pallas_call x1, Pallas kernels, per_device(): pl.pallas_call(finish, out_shape=(jax.ShapeDtypeStruct((edge, edge), F32)...  1.79 us

commit v1 on v0

--- a/solution.py
+++ b/solution.py
@@ -41,10 +41,10 @@
     emb_col_hbm,
     proj_row_hbm,
     proj_col_hbm,
-    pair_out,
-    pair_bias,
+    pair_out_hbm,
+    pair_bias_hbm,
     conv_weight_hbm,
-    conv_bias,
+    conv_bias_hbm,
     target,
     kept,
     loss_out,
@@ -54,6 +54,9 @@
     proj_row,
     proj_col,
     conv_weight,
+    pair_out,
+    pair_bias,
+    conv_bias,
     in_sem,
     rowtail,
     coltail,
@@ -74,6 +77,7 @@
     bias_acc,
     part,
     reduced,
+    whole,
     target_sem,
     row_send,
     row_recv,
@@ -88,7 +92,7 @@
     ag_send,
     ag_recv,
 ):
-    n_row, n_col, n_rep, edge, chan, chunk = sizes
+    n_row, n_col, n_rep, edge, chan, n_own, first_own, chunk = sizes
     n_all = n_row * n_col * n_rep
     pairs = edge // 2
     row, col, rep = lax.axis_index("row"), lax.axis_index("col"), lax.axis_index("rep")
@@ -97,16 +101,19 @@
     me = line * n_col + col
 
     def device(index):
-        across = index % n_col
-        along = index // n_col
-        return {"row": along // n_rep, "rep": along % n_rep, "col": across}
+        across = lax.rem(index, n_col)
+        along = lax.div(index, n_col)
+        return {"row": lax.div(along, n_rep), "rep": lax.rem(along, n_rep), "col": across}
+
+    def await_bytes(ref, sem):
+        pltpu.make_async_copy(ref, ref, sem).wait()
 
     barrier = pltpu.get_barrier_semaphore()
     loop(
         1,
         n_all,
         lambda d: pl.semaphore_signal(
-            barrier, inc=1, device_id=device((me + d) % n_all), device_id_type=MESH
+            barrier, inc=1, device_id=device(lax.rem(me + d, n_all)), device_id_type=MESH
         ),
     )
 
@@ -119,6 +126,9 @@
                 (emb_col_hbm, emb_col),
                 (proj_col_hbm, proj_col),
                 (conv_weight_hbm, conv_weight),
+                (pair_out_hbm, pair_out),
+                (pair_bias_hbm, pair_bias),
+                (conv_bias_hbm, conv_bias),
             )
         )
     ]
@@ -130,7 +140,6 @@
     def rounded(x):
         return x.astype(BF16).astype(F32)
 
-    keep = kept[0, 0].astype(F32)
     for copy in inputs[2:4]:
         copy.wait()
     part_col = jnp.dot(
@@ -140,6 +149,7 @@
     )
     for copy in inputs[0:2]:
         copy.wait()
+    keep = kept[0, 0].astype(F32)
     part_row = lax.dot_general(
         columns(proj_row, emb_row.shape[1], col, n_col),
         emb_row[...],
@@ -165,20 +175,24 @@
         return pltpu.make_async_remote_copy(
             src_ref=rowbuf.at[src],
             dst_ref=rowbuf.at[src],
-            send_sem=row_send.at[d],
-            recv_sem=row_recv.at[src],
-            device_id={"col": (col + d) % n_col},
+            send_sem=row_send,
+            recv_sem=row_recv,
+            device_id={"col": lax.rem(col + d, n_col)},
             device_id_type=MESH,
         )
 
     def redge_copy(side, d, src):
-        to = (line + (1 if side == 0 else n_line - 1)) % n_line
+        to = lax.rem(line + (1 if side == 0 else n_line - 1), n_line)
         return pltpu.make_async_remote_copy(
             src_ref=rowtail.at[side],
             dst_ref=rowedge.at[side, src],
-            send_sem=redge_send.at[side, d],
-            recv_sem=redge_recv.at[side, src],
-            device_id={"row": to // n_rep, "rep": to % n_rep, "col": (col + d) % n_col},
+            send_sem=redge_send,
+            recv_sem=redge_recv,
+            device_id={
+                "row": lax.div(to, n_rep),
+                "rep": lax.rem(to, n_rep),
+                "col": lax.rem(col + d, n_col),
+            },
             device_id_type=MESH,
         )
 
@@ -186,31 +200,41 @@
         return pltpu.make_async_remote_copy(
             src_ref=colbuf.at[src],
             dst_ref=colbuf.at[src],
-            send_sem=col_send.at[d],
-            recv_sem=col_recv.at[src],
-            device_id={"row": (row + d) % n_row},
+            send_sem=col_send,
+            recv_sem=col_recv,
+            device_id={"row": lax.rem(row + d, n_row)},
             device_id_type=MESH,
         )
 
     def cedge_copy(side, d, src):
-        to = (col + (1 if side == 0 else n_col - 1)) % n_col
+        to = lax.rem(col + (1 if side == 0 else n_col - 1), n_col)
         return pltpu.make_async_remote_copy(
             src_ref=coltail.at[side],
             dst_ref=coledge.at[side, src],
-            send_sem=cedge_send.at[side, d],
-            recv_sem=cedge_recv.at[side, src],
-            device_id={"row": (row + d) % n_row, "col": to},
+            send_sem=cedge_send,
+            recv_sem=cedge_recv,
+            device_id={"row": lax.rem(row + d, n_row), "col": to},
             device_id_type=MESH,
         )
 
-    loop(1, n_row, lambda d: col_copy(d, row).start())
-    loop(1, n_col, lambda d: row_copy(d, col).start())
     for side in range(2):
         loop(0, n_row, lambda d: cedge_copy(side, d, row).start())
+    loop(1, n_row, lambda d: col_copy(d, row).start())
+    for side in range(2):
         loop(0, n_col, lambda d: redge_copy(side, d, col).start())
+    loop(1, n_col, lambda d: row_copy(d, col).start())
+
+    def await_features(col_sem, row_sem, cedge_sem, redge_sem):
+        await_bytes(coledge, cedge_sem)
+        if n_row > 1:
+            await_bytes(colbuf.at[0 : n_row - 1], col_sem)
+        await_bytes(rowedge, redge_sem)
+        if n_col > 1:
+            await_bytes(rowbuf.at[0 : n_col - 1], row_sem)
 
     fetch.wait()
-    inputs[4].wait()
+    for copy in inputs[4:]:
+        copy.wait()
 
     def widen(c, _):
         start = pl.multiple_of(c * edge, edge)
@@ -235,11 +259,7 @@
     bias_acc[...] = jnp.zeros_like(bias_acc)
     total[...] = jnp.zeros_like(total)
 
-    loop(1, n_row, lambda d: col_copy(d, (row + n_row - d) % n_row).wait_recv())
-    loop(1, n_col, lambda d: row_copy(d, (col + n_col - d) % n_col).wait_recv())
-    for side in range(2):
-        loop(0, n_row, lambda d: cedge_copy(side, d, (row + n_row - d) % n_row).wait_recv())
-        loop(0, n_col, lambda d: redge_copy(side, d, (col + n_col - d) % n_col).wait_recv())
+    await_features(col_recv, row_recv, cedge_recv, redge_recv)
 
     def summed(terms):
         return sum(x.astype(F32) for x in terms)
@@ -377,67 +397,89 @@
         preferred_element_type=F32,
     )
     part[0:rows, :] = flat
-    part[rows : rows + 8, :] = jnp.concatenate([bias_sum, bias_sum], axis=1)
-    rest = n_all * chunk - rows - 8
+    for term in range(3):
+        low = rows + 8 * term
+        part[low : low + 8, :] = jnp.concatenate([bias_sum, bias_sum], axis=1)
+    rest = n_own * chunk - rows - 24
     if rest > 0:
-        part[rows + 8 :, :] = jnp.zeros((rest, 128), F32)
+        part[rows + 24 :, :] = jnp.zeros((rest, 128), F32)
+
+    mine = me - first_own
+    owner = (mine >= 0) & (mine < n_own)
 
     def piece(index):
         return pl.ds(pl.multiple_of(index * chunk, 8), chunk)
 
-    def rs_copy(d, to, src):
-        return pltpu.make_async_remote_copy(
-            src_ref=part.at[piece(to)],
-            dst_ref=reduced.at[src],
-            send_sem=rs_send.at[d],
-            recv_sem=rs_recv.at[src],
-            device_id=device(to),
+    def scatter(d):
+        index = lax.rem(me + d, n_own)
+
+        @pl.when(first_own + index != me)
+        def _():
+            pltpu.make_async_remote_copy(
+                src_ref=part.at[piece(index)],
+                dst_ref=reduced.at[me],
+                send_sem=rs_send,
+                recv_sem=rs_recv,
+                device_id=device(first_own + index),
+                device_id_type=MESH,
+            ).start()
+
+    def gather(d):
+        pltpu.make_async_remote_copy(
+            src_ref=full.at[mine],
+            dst_ref=full.at[mine],
+            send_sem=ag_send,
+            recv_sem=ag_recv,
+            device_id=device(lax.rem(me + d, n_all)),
             device_id_type=MESH,
-        )
-
-    def ag_copy(d, to, src):
-        return pltpu.make_async_remote_copy(
-            src_ref=full.at[src],
-            dst_ref=full.at[src],
-            send_sem=ag_send.at[d],
-            recv_sem=ag_recv.at[src],
-            device_id=device(to),
-            device_id_type=MESH,
-        )
-
-    loop(1, n_all, lambda d: rs_copy(d, (me + d) % n_all, me).start())
-    reduced[me] = part[piece(me), :]
-    loop(1, n_all, lambda d: rs_copy(d, (me + d) % n_all, (me + n_all - d) % n_all).wait_recv())
-    if n_all <= 16:
-        own = sum(reduced[r] for r in range(n_all))
-    else:
-        own = lax.fori_loop(
-            0, n_all, lambda r, x: x + reduced[r], jnp.zeros((chunk, 128), F32)
-        )
-    full[me] = own
-    loop(1, n_all, lambda d: ag_copy(d, (me + d) % n_all, me).start())
-    loop(1, n_all, lambda d: ag_copy(d, (me + d) % n_all, (me + n_all - d) % n_all).wait_recv())
-
-    loop(1, n_row, lambda d: col_copy(d, row).wait_send())
-    loop(1, n_col, lambda d: row_copy(d, col).wait_send())
-    for side in range(2):
-        loop(0, n_row, lambda d: cedge_copy(side, d, row).wait_send())
-        loop(0, n_col, lambda d: redge_copy(side, d, col).wait_send())
-    loop(1, n_all, lambda d: rs_copy(d, (me + d) % n_all, me).wait_send())
-    loop(1, n_all, lambda d: ag_copy(d, (me + d) % n_all, me).wait_send())
-
-
-def finish(loss_in, gathered, loss_out, conv_grad_out, bias_out, full):
+        ).start()
+
+    loop(0, n_own, scatter)
+
+    @pl.when(owner)
+    def _():
+        reduced[me] = part[piece(mine), :]
+        await_bytes(reduced.at[0 : n_all - 1], rs_recv)
+        if n_all <= 16:
+            own = sum(reduced[r] for r in range(n_all))
+        else:
+            own = lax.fori_loop(
+                0, n_all, lambda r, x: x + reduced[r], jnp.zeros((chunk, 128), F32)
+            )
+        at = mine * chunk + lax.broadcasted_iota(jnp.int32, (chunk, 128), 0)
+        second = own - rounded(own)
+        third = second - rounded(second)
+        own = jnp.where(at >= rows + 8, jnp.where(at >= rows + 16, third, second), own)
+        full[mine] = own.astype(BF16)
+        loop(1, n_all, gather)
+        if n_own > 1:
+            await_bytes(full.at[0 : n_own - 1], ag_recv)
+            await_bytes(part.at[0 : (n_own - 1) * chunk], rs_send)
+
+    @pl.when(jnp.logical_not(owner))
+    def _():
+        await_bytes(full, ag_recv)
+        await_bytes(part, rs_send)
+
+    await_features(col_send, row_send, cedge_send, redge_send)
+
+    @pl.when(owner)
+    def _():
+        await_bytes(whole, ag_send)
+
+
+def finish(loss, gathered, loss_hbm, conv_grad_hbm, bias_hbm, full, conv_grad_out, bias_out, sem):
     n_all, chunk = gathered.shape[0:2]
+    loss_copy = pltpu.make_async_copy(loss, loss_hbm, sem.at[0])
+    loss_copy.start()
 
     def place(r):
-        full[pl.ds(r * chunk, chunk), :] = gathered[r]
+        full[pl.ds(r * chunk, chunk), :] = gathered[r].astype(F32)
 
     loop(0, n_all, place)
     chan = bias_out.shape[1]
     half = 3 * chan // 2
     rows = 3 * chan + half
-    loss_out[...] = loss_in[...]
     for b in range(3):
         low = b * chan
         conv_grad_out[2, b] = full[low : low + chan, 0:chan]
@@ -447,7 +489,14 @@
     conv_grad_out[0, 1, 0 : half - chan] = full[low + chan : low + half, 0:chan]
     conv_grad_out[0, 1, half - chan :] = full[low : low + 2 * chan - half, chan : 2 * chan]
     conv_grad_out[0, 2] = full[low + 2 * chan - half : low + half, chan : 2 * chan]
-    bias_out[...] = full[rows : rows + 1, 0:chan]
+    bias_out[...] = sum(full[rows + 8 * t : rows + 8 * t + 1, 0:chan] for t in range(3))
+    grad_copy = pltpu.make_async_copy(conv_grad_out, conv_grad_hbm, sem.at[1])
+    bias_copy = pltpu.make_async_copy(bias_out, bias_hbm, sem.at[2])
+    grad_copy.start()
+    bias_copy.start()
+    loss_copy.wait()
+    grad_copy.wait()
+    bias_copy.wait()
 
 
 def solution(mesh):
@@ -469,21 +518,24 @@
         chan, edge = target.shape[0], target.shape[1]
         rank = pair_out.shape[0]
         pairs = edge // 2
-        used = 3 * chan + 3 * chan // 2 + 8
-        chunk = 8 * pl.cdiv(used, 8 * n_all)
+        used = 3 * chan + 3 * chan // 2 + 24
+        inner = n_row // 2 if n_row >= 4 else n_row
+        n_own = inner * n_col * n_rep
+        first_own = (n_row - inner) // 2 * n_col * n_rep
+        chunk = 8 * pl.cdiv(used, 8 * n_own)
 
         dma = pltpu.SemaphoreType.DMA
         vmem = pl.BlockSpec(memory_space=pltpu.VMEM)
-        hbm = pl.BlockSpec(memory_space=pl.ANY)
+        hbm = pl.BlockSpec(memory_space=pltpu.HBM)
         loss, sums = pl.pallas_call(
-            functools.partial(kernel, (n_row, n_col, n_rep, edge, chan, chunk)),
+            functools.partial(
+                kernel, (n_row, n_col, n_rep, edge, chan, n_own, first_own, chunk)
+            ),
             out_shape=(
-                jax.ShapeDtypeStruct((edge, edge), F32),
-                jax.ShapeDtypeStruct((n_all, chunk, 128), F32),
+                pltpu.VMEM((edge, edge), F32),
+                pltpu.VMEM((n_own, chunk, 128), BF16),
             ),
-            in_specs=[hbm] * 4
-            + [vmem] * 2
-            + [hbm, vmem, hbm, pl.BlockSpec(memory_space=pltpu.SMEM)],
+            in_specs=[hbm] * 9 + [pl.BlockSpec(memory_space=pltpu.SMEM)],
             out_specs=(vmem,) * 2,
             scratch_shapes=[
                 pltpu.VMEM(emb_row.shape, BF16),
@@ -491,7 +543,10 @@
                 pltpu.VMEM(proj_row.shape[::-1], BF16),
                 pltpu.VMEM(proj_col.shape[::-1], BF16),
                 pltpu.VMEM(conv_weight.shape, BF16),
-                dma((5,)),
+                pltpu.VMEM(pair_out.shape, BF16),
+                pltpu.VMEM((1, chan), F32),
+                pltpu.VMEM((1, chan), F32),
+                dma((8,)),
                 pltpu.VMEM((2, 16, rank), F32),
                 pltpu.VMEM((2, 8, rank), F32),
                 pltpu.VMEM((n_col, rank + 16, edge), BF16),
@@ -509,21 +564,10 @@
                 pltpu.VMEM((3 * chan, 3 * chan), F32),
                 pltpu.VMEM((3 * chan, 3 * chan), F32),
                 pltpu.VMEM((chan, 2 * edge), F32),
-                pltpu.VMEM((n_all * chunk, 128), F32),
+                pltpu.VMEM((n_own * chunk, 128), F32),
                 pltpu.VMEM((n_all, chunk, 128), F32),
-                pltpu.SemaphoreType.DMA,
-                dma((n_col,)),
-                dma((n_col,)),
-                dma((2, n_col)),
-                dma((2, n_col)),
-                dma((n_row,)),
-                dma((n_row,)),
-                dma((2, n_row)),
-                dma((2, n_row)),
-                dma((n_all,)),
-                dma((n_all,)),
-                dma((n_all,)),
-                dma((n_all,)),
+                pltpu.VMEM((n_all - 1, chunk, 128), BF16),
+                *[pltpu.SemaphoreType.DMA] * 13,
             ],
             compiler_params=pltpu.CompilerParams(collective_id=0, has_side_effects=True),
             name="pair_step",
@@ -547,10 +591,17 @@
                 jax.ShapeDtypeStruct((1, chan), F32),
             ),
             in_specs=[vmem] * 2,
-            out_specs=(vmem,) * 3,
-            scratch_shapes=[pltpu.VMEM((n_all * chunk, 128), F32)],
+            out_specs=(hbm,) * 3,
+            scratch_shapes=[
+                pltpu.VMEM((n_own * chunk, 128), F32),
+                pltpu.VMEM((3, 3, chan, chan), F32),
+                pltpu.VMEM((1, chan), F32),
+                dma((3,)),
+            ],
             name="finish",
-        )(loss, sums)
+        )(
+            *(pltpu.with_memory_space_constraint(x, pltpu.VMEM) for x in (loss, sums))
+        )
         return loss, grads, bias.reshape(chan)
 
     in_specs = (

time: 39.7 us -> 35.1 us (0.88)
  the two profiles are of different devices: /device:TPU:1 before, /device:TPU:0 now
where the time goes in v1:
time: 35.1 us; the launch traced here: 35 us
  Pallas kernels  33.7 us (96%)
  between operations  1.29 us (4%)
    pallas_call x1, Pallas kernels, per_device(): pl.pallas_call(functools.partial(kernel, (n_row, n_col, n_rep, edge, chan...  32.8 us
    pallas_call x1, Pallas kernels, per_device(): pl.pallas_call(finish, out_shape=(jax.ShapeDtypeStruct((edge, edge), F32)...  0.83 us

profile of v1, /device:TPU:0, one launch (start us, length us, event | category | flops | bytes accessed | tf_op | source)
XLA Modules:
  0.0 35.0 jit_solution(3908305159695820941)
XLA Ops:
  1.3 32.8 %pair_step.1 = (f32[128,128]{1,0:T(8,128)S(1)}, bf16[8,40,128]{2,1,0:T(8,128)(2,1)S(1)}) custom-call(bf16[128,640]{1,0:T(8,128)(2,1)} %emb_row_hbm.1, bf16[320,128]{1,0:T(8,128)(2,1)} %bitcast.8, bf16[64,1280]{1,0:T(8,128)(2,1)} %bitcast.6, bf16[64,1280]{1,0:T(8,128)(2,1)} %bitcast.7, bf16[64,64]{1,0:T(8,128)(2,1)} %pair_out_hbm.1, f32[1,64]{1,0:T(1,128)} %bitcast.9, ...), custom_call_target="tpu_custom_call" | custom-call | tf_op jit(solution)/shard_map/pair_step/pallas_call | solution.py:530
  34.1 0.8 %finish.1 = (f32[128,128]{1,0:T(8,128)}, f32[3,3,64,64]{3,2,1,0:T(8,128)}, f32[1,64]{1,0:T(1,128)}) custom-call(f32[128,128]{1,0:T(8,128)S(1)} %get-tuple-element.8.loss, bf16[8,40,128]{2,1,0:T(8,128)(2,1)S(1)} %get-tuple-element.9.gathered), custom_call_target="tpu_custom_call" | custom-call | tf_op jit(solution)/shard_map/finish/pallas_call | solution.py:586

commit v2 on v1

--- a/solution.py
+++ b/solution.py
@@ -32,7 +32,30 @@
         tile = jnp.minimum(tile, (everything - window) // 128)
     value = ref[:, pl.ds(pl.multiple_of(tile * 128, 128), window)].astype(F32)
     shift = window - (index * width - tile * 128)
-    return pltpu.roll(value, shift % window, 1)[:, 0:width].astype(BF16)
+    value = pltpu.roll(value, lax.rem(shift, window), 1)
+    lane = lax.broadcasted_iota(jnp.int32, value.shape, 1)
+    return jnp.where(lane < width, value, 0.0).astype(BF16)
+
+
+def padded(value, square):
+    if all(have == 256 or have % 128 == 0 for have in value.shape):
+        for axis in range(2):
+            if value.shape[axis] < 256:
+                blank = list(value.shape)
+                blank[axis] = 256 - blank[axis]
+                value = jnp.concatenate([value, jnp.zeros(blank, BF16)], axis=axis)
+        return value
+    square[...] = jnp.zeros_like(square)
+    square[0 : value.shape[0], 0 : value.shape[1]] = value
+    return square[...]
+
+
+def wide_tile(value, low):
+    value = value[:, low : low + 256]
+    if value.shape[1] < 256:
+        blank = jnp.zeros((value.shape[0], 256 - value.shape[1]), BF16)
+        value = jnp.concatenate([value, blank], axis=1)
+    return value
 
 
 def kernel(
@@ -66,9 +89,13 @@
     coledge,
     row_feat,
     col_wide,
-    wide_t,
+    feat_pairs,
+    square,
+    wide,
+    weight_t,
     target_in,
     target32,
+    aims,
     hid,
     base,
     grad_in,
@@ -142,21 +169,29 @@
 
     for copy in inputs[2:4]:
         copy.wait()
-    part_col = jnp.dot(
-        columns(proj_col, emb_col.shape[0], row, n_row),
-        emb_col[...],
-        preferred_element_type=F32,
+    rank = proj_row.shape[0]
+
+    def project(col_sum, row_sum):
+        width = emb_col.shape[0]
+        left = columns(proj_col, width, row, n_row)
+        for low in range(0, width, 256):
+            right = padded(emb_col[low : min(low + 256, width), :], square)
+            pltpu.matmul_push_rhs(right, 0, 0)
+            pltpu.matmul_acc_lhs(col_sum, wide_tile(left, low), load_staged_rhs=0)
+        for copy in inputs[0:2]:
+            copy.wait()
+        width = emb_row.shape[1]
+        left = columns(proj_row, width, col, n_col)
+        for low in range(0, width, 256):
+            right = padded(emb_row[:, low : min(low + 256, width)], square)
+            pltpu.matmul_push_rhs(right, 0, 1, transpose=True)
+            pltpu.matmul_acc_lhs(row_sum, wide_tile(left, low), load_staged_rhs=0)
+        return pltpu.matmul_pop(col_sum)[:, 0:edge], pltpu.matmul_pop(row_sum)[:, 0:edge]
+
+    part_col, part_row = pl.run_scoped(
+        project, *[pltpu.ACC(unit)((rank, 256), F32) for unit in range(2)]
     )
-    for copy in inputs[0:2]:
-        copy.wait()
     keep = kept[0, 0].astype(F32)
-    part_row = lax.dot_general(
-        columns(proj_row, emb_row.shape[1], col, n_col),
-        emb_row[...],
-        NT,
-        preferred_element_type=F32,
-    )
-    rank = part_row.shape[0]
     colbuf[row] = part_col.astype(BF16)
     rowbuf[col, 0:rank, :] = part_row.astype(BF16)
     rowbuf[col, rank:, :] = jnp.full((16, edge), keep, F32).astype(BF16)
@@ -242,22 +277,39 @@
         return 0
 
     lax.fori_loop(0, chan, widen, 0, unroll=4)
+    def lay(p, _):
+        for r in range(2):
+            aim = target32[pl.ds(2 * p + r, chan, stride=edge), :].astype(BF16)
+            start = pl.multiple_of(p * chan, chan)
+            aims[pl.ds(start, chan), r * edge : (r + 1) * edge] = aim
+        return 0
+
+    lax.fori_loop(0, pairs, lay, 0, unroll=2)
     for a in range(3):
         for b in range(3):
             weight_f[b * chan : (b + 1) * chan, a * chan : (a + 1) * chan] = conv_weight[
                 a, b
             ].astype(F32)
-    weight_t = weight_f[...].T.astype(BF16)
+    turned = weight_f[...].T
+    eye = lax.broadcasted_iota(jnp.int32, (chan, chan), 0) == lax.broadcasted_iota(
+        jnp.int32, (chan, chan), 1
+    )
+    none = jnp.zeros((chan, chan), F32)
+    minus = jnp.concatenate([none, jnp.where(eye, -1.0, 0.0), none], axis=0)
+    weight_t[...] = jnp.concatenate([turned, minus], axis=1).astype(BF16)
     out_t = pair_out[...].astype(F32).T
+    out_t = jnp.concatenate([out_t, out_t], axis=1)
     pair_b = jnp.broadcast_to(pair_bias[...], (128, chan)).T
     conv_b = jnp.broadcast_to(conv_bias[...], (128, chan)).T
-    zeros = jnp.zeros((2 * chan, 2 * edge), BF16)
-    grad_in[0 : 2 * chan, :] = zeros
-    grad_in[(pairs + 2) * chan : (pairs + 4) * chan, :] = zeros
-    base[0 : 2 * chan, :] = zeros.astype(F32)
-    base[(pairs + 2) * chan : (pairs + 4) * chan, :] = zeros.astype(F32)
+    term = lax.broadcasted_iota(jnp.int32, (chan, 128), 1)
+    second = pair_b - rounded(pair_b)
+    third = second - rounded(second)
+    bias_terms = jnp.where(
+        term == 0,
+        pair_b,
+        jnp.where(term == 1, second, jnp.where(term == 2, third, 0.0)),
+    ).astype(BF16)
     bias_acc[...] = jnp.zeros_like(bias_acc)
-    total[...] = jnp.zeros_like(total)
 
     await_features(col_recv, row_recv, cedge_recv, redge_recv)
 
@@ -270,13 +322,12 @@
     col_wide[0:8, :] = summed(coledge[0, r] for r in range(n_row))
     col_wide[8 : edge + 8, :] = summed(colbuf[r] for r in range(n_row)).T
     col_wide[edge + 8 :, :] = summed(coledge[1, r] for r in range(n_row))
-    for b in range(3):
-        wide_t[b * edge : (b + 1) * edge, :] = col_wide[
-            6 + 2 * b : 6 + 2 * b + edge, :
-        ].astype(BF16)
+    feat_pairs[0 : pairs + 2, :] = jnp.concatenate(
+        [row_feat[pl.ds(6 + r, pairs + 2, stride=2), :] for r in range(2)], axis=1
+    )
 
     lane = lax.broadcasted_iota(jnp.int32, (1, edge), 1)
-    before, after = (col + n_col - 1) % n_col, (col + 1) % n_col
+    before, after = lax.rem(col + n_col - 1, n_col), lax.rem(col + 1, n_col)
     has_before = (col > 0).astype(F32)
     has_after = (col < n_col - 1).astype(F32)
 
@@ -291,92 +342,234 @@
     middle = masks(lambda c: rowbuf[c, rank:, 0:1].astype(F32)[0:1], jnp.float32(1))
     bottom = masks(lambda c: rowedge[1, c, 8:9, 0:1], (line < n_line - 1).astype(F32))
 
-    def features(pair, count, mask, inner):
-        scaled = []
-        for r in range(2 * count):
-            feat = row_feat[pl.ds(2 * pair + 8 + r, 1), :]
-            scaled.append((out_t * feat).astype(BF16))
-        product = lax.dot_general(
-            jnp.concatenate(scaled, axis=0), wide_t[...], NT, preferred_element_type=F32
-        )
-        for r in range(2 * count):
-            p = pair + r // 2
-            lanes = slice((r % 2) * edge, (r % 2 + 1) * edge)
-            for b in range(3):
-                value = product[r * chan : (r + 1) * chan, b * edge : (b + 1) * edge] + pair_b
-                start = pl.multiple_of((p + 1) * 3 * chan + b * chan, chan)
-                hid[pl.ds(start, chan), lanes] = (jnp.maximum(value, 0.0) * mask[b]).astype(BF16)
-                if inner and b == 1:
-                    aim = target32[pl.ds(2 * pair + r, chan, stride=edge), :]
-                    start = pl.multiple_of((p + 2) * chan, chan)
-                    base[pl.ds(start, chan), lanes] = (value + conv_b) - aim
-
-    features(-1, 1, top, False)
-    features(pairs, 1, bottom, False)
-    group = 4
-
-    def conv_of(p):
-        start = pl.multiple_of((p + 1) * 3 * chan, 3 * chan)
-        return jnp.dot(weight_t, hid[pl.ds(start, 3 * chan), :], preferred_element_type=F32)
-
-    def slot(p):
-        return pl.ds(pl.multiple_of((p + 2) * chan, chan), chan)
-
-    def spread(p, done):
-        y = conv_of(p)
-        base[slot(p + 1), :] += y[0:chan]
-        base[slot(p), :] += y[chan : 2 * chan]
-        if done:
-            differ = (base[slot(p - 1), :] + y[2 * chan :]) * keep
-            grad_in[slot(p - 1), :] = differ.astype(BF16)
-            bias_acc[...] += differ
-            loss = 0.5 * jnp.sum(differ * differ, axis=0, keepdims=True)
-            loss_out[pl.ds(2 * (p - 1), 1), :] = loss[:, 0:edge]
-            loss_out[pl.ds(2 * (p - 1) + 1, 1), :] = loss[:, edge : 2 * edge]
-
-    def grads(first, count):
-        value = total[...]
-        for r in range(count):
-            p = first + r
-            start = pl.multiple_of((p + 1) * 3 * chan, 3 * chan)
-            near = pl.multiple_of((p + 1) * chan, chan)
-            value = value + lax.dot_general(
-                hid[pl.ds(start, 3 * chan), :],
-                grad_in[pl.ds(near, 3 * chan), :],
-                NT,
-                preferred_element_type=F32,
+    shifted = [col_wide[6 + 2 * b : 6 + 2 * b + edge, :].T for b in range(3)]
+    first_rows = lax.broadcasted_iota(jnp.int32, (2 * edge - 2 * rank, 2 * edge), 0) < 3
+
+    def operand(b, mask):
+        value = shifted[b] * mask
+        blank = jnp.zeros_like(value)
+        ones = jnp.where(first_rows, jnp.concatenate([mask, mask], axis=1), 0.0)
+        return jnp.concatenate(
+            [
+                jnp.concatenate([value, blank], axis=1),
+                jnp.concatenate([blank, value], axis=1),
+                ones,
+            ],
+            axis=0,
+        ).astype(BF16)
+
+    for b in range(3):
+        wide[b] = operand(b, middle[b])
+
+    def scaled(p, count):
+        low = (out_t * feat_pairs[pl.ds(p + 1 + r, 1), :] for r in range(count))
+        low = jnp.concatenate([x.astype(BF16) for x in low], axis=0)
+        return jnp.concatenate([low, jnp.concatenate([bias_terms] * count, axis=0)], axis=1)
+
+    conv_b = jnp.concatenate([conv_b, conv_b], axis=1)
+    blank = jnp.zeros((chan, 2 * edge), BF16)
+
+    def slot(offset, first=0, count=1, of=1):
+        low = (offset % 16 * of + first) * chan
+        return slice(low, low + count * chan)
+
+    def inside(p, offset):
+        return not isinstance(p, int) or 0 <= p + offset < pairs
+
+    def finish_pair(p, offset, conv):
+        differ = (base[slot(offset), :] + conv) * keep
+        grad_in[slot(offset), :] = differ.astype(BF16)
+        bias_acc[...] += differ
+        loss = 0.5 * jnp.sum(differ * differ, axis=0, keepdims=True)
+        at = 2 * (p + offset)
+        loss_out[pl.ds(at, 1), :] = loss[:, 0:edge]
+        loss_out[pl.ds(at + 1, 1), :] = loss[:, edge : 2 * edge]
+
+    def main(sum0, sum1, sum2, sum3, left0, left1, mid0, mid1, spare0, grad0, right0, right1, spare1, halo, grad1):
+        sums, lefts, mids, rights = (
+            (sum0, sum1, sum2, sum3),
+            (left0, left1),
+            (mid0, mid1),
+            (right0, right1),
+        )
+        spares, grads = (spare0, spare1), (grad0, grad1)
+        stage = [0, 0]
+
+        def push_wide(unit, b):
+            return lambda at: pltpu.matmul_push_rhs(wide[b], at, unit)
+
+        def halo_item(p, offset, b, mask):
+            def push(at):
+                pltpu.matmul_push_rhs(operand(b, mask[b]), at, 1)
+
+            def go(at):
+                pltpu.matmul_acc_lhs(halo, scaled(p + offset, 1), load_staged_rhs=at)
+                value = jnp.maximum(pltpu.matmul_pop(halo), 0.0)
+                hid[slot(offset, b, 1, 3), :] = value.astype(BF16)
+
+            return push, go, None, 4
+
+        def feature_item(unit, b, p, offset, acc, memo):
+            def go(at):
+                if offset not in memo:
+                    memo[offset] = scaled(p + offset, 2)
+                pltpu.matmul_acc_lhs(acc, memo[offset], load_staged_rhs=at)
+
+            def after():
+                value = pltpu.matmul_pop(acc)
+                for r in range(2):
+                    own = value[r * chan : (r + 1) * chan]
+                    hid[slot(offset + r, b, 1, 3), :] = jnp.maximum(own, 0.0).astype(BF16)
+                    if b == 1:
+                        base[slot(offset + r), :] = own + conv_b
+
+            return push_wide(unit, b), go, after, 8
+
+        def conv_item(p, offset):
+            taps = [a for a in range(3) if inside(p, offset + 1 - a)]
+
+            def push(at):
+                aim = blank
+                if inside(p, offset):
+                    aim = aims[pl.ds(pl.multiple_of((p + offset) * chan, chan), chan), :]
+                right = jnp.concatenate([hid[slot(offset, 0, 3, 3), :], aim], axis=0)
+                pltpu.matmul_push_rhs(right, at, 0)
+
+            def go(at):
+                for a in taps:
+                    pltpu.matmul_acc_lhs(
+                        sums[(offset + 1 - a) % 4],
+                        weight_t[a * chan : (a + 1) * chan, :],
+                        load_staged_rhs=at,
+                    )
+                    at = None
+
+            def after():
+                if 2 in taps:
+                    finish_pair(p, offset - 1, pltpu.matmul_pop(sums[(offset - 1) % 4]))
+
+            return push, go, after, 4 * len(taps)
+
+        def grad_item(unit, p, offset):
+            def push(at):
+                right = [
+                    grad_in[slot(offset + k), :] if inside(p, offset + k) else blank
+                    for k in range(-2, 2)
+                ]
+                right = jnp.concatenate(right, axis=0)
+                pltpu.matmul_push_rhs(right, at, unit, transpose=True)
+
+            def go(at):
+                left = hid[slot(offset, 0, 3, 3), :]
+                pltpu.matmul_acc_lhs(grads[unit], left, load_staged_rhs=at)
+
+            return push, go, None, 12
+
+        def spare_item(unit, b):
+            def go(at):
+                left = jnp.zeros((16, 2 * edge), BF16)
+                pltpu.matmul_acc_lhs(spares[unit], left, load_staged_rhs=at)
+
+            def after():
+                part[0:16, :] = pltpu.matmul_pop(spares[unit])[:, 0:128]
+
+            return push_wide(unit, b), go, after, 1
+
+        def run(queues, tails=(None, None), primed=True):
+            spent, at, waiting = [0, 0], [0, 0], []
+            for unit in range(2):
+                if queues[unit] and not primed:
+                    queues[unit][0][0](stage[unit])
+            while any(at[u] < len(queues[u]) for u in range(2)):
+                unit = min(
+                    (u for u in range(2) if at[u] < len(queues[u])), key=lambda u: spent[u]
+                )
+                queue, index = queues[unit], at[unit]
+                _, go, after, cost = queue[index]
+                later = queue[index + 1][0] if index + 1 < len(queue) else tails[unit]
+                while len(waiting) > 1:
+                    waiting.pop(0)()
+                go(stage[unit])
+                stage[unit] = 1 - stage[unit]
+                if later is not None:
+                    later(stage[unit])
+                at[unit] += 1
+                spent[unit] += cost
+                if after is not None:
+                    waiting.append(after)
+            for after in waiting:
+                after()
+
+        tails = (push_wide(0, 0), push_wide(1, 2))
+
+        def features(p, low):
+            memo = {}
+            first, second = [], []
+            for half in range(2):
+                offset = low + 2 * half
+                first.append(feature_item(0, 0, p, offset, lefts[half], memo))
+                first.append(feature_item(0, 1, p, offset, mids[half], memo))
+                second.append(feature_item(1, 2, p, offset, rights[half], memo))
+            return first, second
+
+        def merged(own, other):
+            return own[0:2] + other[0:2] + own[2:4] + other[2:]
+
+        def group(p, low):
+            f0, f1 = features(p, low)
+            convs = [conv_item(p, low - 4 + r) for r in range(4)]
+            turns = [grad_item(1, p, low - 12 + r) for r in range(4)]
+            run((merged(f0, convs), [f1[0], *turns[0:2], f1[1], *turns[2:4]]), tails)
+
+        halos = [halo_item(0, -1, b, top) for b in range(3)]
+        f0, f1 = features(0, 0)
+        run((f0, halos + f1), tails, primed=False)
+        f0, f1 = features(0, 4)
+        convs = [conv_item(0, r) for r in range(-1, 4)]
+        run((merged(f0, convs) + [spare_item(0, 0)], f1), tails)
+        f0, f1 = features(0, 8)
+        convs = [conv_item(0, r) for r in range(4, 8)]
+        turns = [grad_item(1, 0, r) for r in (-1, 0, 1)]
+        run((merged(f0, convs), [f1[0], *turns[0:2], f1[1], turns[2], spare_item(1, 2)]), tails)
+        f0, f1 = features(0, 12)
+        convs = [conv_item(0, r) for r in range(8, 12)]
+        turns = [grad_item(1, 0, r) for r in (2, 3)]
+        run((merged(f0, convs), [f1[0], turns[0], f1[1], turns[1]]), tails)
+
+        def step(t, _):
+            p = pl.multiple_of(t * 16, 16)
+            for k in range(4):
+                group(p, 4 * k)
+            return 0
+
+        lax.fori_loop(1, pairs // 16, step, 0)
+        halos = [halo_item(pairs, 0, b, bottom) for b in range(3)]
+        turns = [grad_item(1, pairs, r) for r in range(-12, -6)]
+        convs = [conv_item(pairs, r) for r in range(-4, 1)]
+        run(
+            (
+                [spare_item(0, 0)] + convs,
+                [spare_item(1, 2)] + halos + turns,
             )
-        total[...] = value
-
-    for g in range(3):
-        features(g * group, group, middle, True)
-    spread(-1, False)
-    spread(0, False)
-    for r in range(group):
-        spread(1 + r, True)
-    lag = 2 * group - 1
-
-    def step(g, _):
-        grads(g * group - 3 * group - 1, group)
-        for r in range(group):
-            spread(g * group - lag + r, True)
-        features(g * group, group, middle, True)
-        return 0
-
-    lax.fori_loop(3, pairs // group, step, 0)
-
-    def conv_step(g, _):
-        for r in range(group):
-            spread(pairs - lag + g * group + r, True)
-        return 0
-
-    lax.fori_loop(0, 2, conv_step, 0)
-
-    def grad_step(g, _):
-        grads(pairs - 3 * group - 1 + g * 7, 7)
-        return 0
-
-    lax.fori_loop(0, 2, grad_step, 0)
+        )
+        turns = [[grad_item(u, pairs, r) for r in range(-6 + u, 1, 2)] for u in range(2)]
+        run(turns, primed=False)
+        total[...] = pltpu.matmul_pop(grad0) + pltpu.matmul_pop(grad1)
+
+    def accumulator(unit, rows_of):
+        return pltpu.ACC(unit)((rows_of, 2 * edge), F32)
+
+    pl.run_scoped(
+        main,
+        *[accumulator(0, chan)] * 4,
+        *[accumulator(0, 2 * chan)] * 4,
+        accumulator(0, 16),
+        accumulator(0, 3 * chan),
+        *[accumulator(1, 2 * chan)] * 2,
+        accumulator(1, 16),
+        accumulator(1, chan),
+        accumulator(1, 3 * chan),
+    )
 
     norm = 1.0 / (edge * edge)
     half = 3 * chan // 2
@@ -384,18 +577,16 @@
     sums = total[...] * norm
     flat = jnp.concatenate(
         [
-            sums[:, 0 : 2 * chan],
-            jnp.concatenate([sums[0:half, 2 * chan :], sums[half:, 2 * chan :]], axis=1),
+            sums[:, 2 * chan :],
+            jnp.concatenate(
+                [sums[0:half, chan : 2 * chan], sums[half:, chan : 2 * chan]], axis=1
+            ),
         ],
         axis=0,
     )
-    bias_sum = lax.dot_general(
-        jnp.ones((8, 2 * edge), F32),
-        bias_acc[...] * norm,
-        NT,
-        precision=lax.Precision.HIGHEST,
-        preferred_element_type=F32,
-    )
+    bias_sum = (bias_acc[:, 0:edge] + bias_acc[:, edge:]).T
+    bias_sum = jnp.sum(bias_sum, axis=0, keepdims=True) * norm
+    bias_sum = jnp.broadcast_to(bias_sum, (8, chan))
     part[0:rows, :] = flat
     for term in range(3):
         low = rows + 8 * term
@@ -482,13 +673,13 @@
     rows = 3 * chan + half
     for b in range(3):
         low = b * chan
-        conv_grad_out[2, b] = full[low : low + chan, 0:chan]
-        conv_grad_out[1, b] = full[low : low + chan, chan : 2 * chan]
+        conv_grad_out[1, b] = full[low : low + chan, 0:chan]
+        conv_grad_out[0, b] = full[low : low + chan, chan : 2 * chan]
     low = 3 * chan
-    conv_grad_out[0, 0] = full[low : low + chan, 0:chan]
-    conv_grad_out[0, 1, 0 : half - chan] = full[low + chan : low + half, 0:chan]
-    conv_grad_out[0, 1, half - chan :] = full[low : low + 2 * chan - half, chan : 2 * chan]
-    conv_grad_out[0, 2] = full[low + 2 * chan - half : low + half, chan : 2 * chan]
+    conv_grad_out[2, 0] = full[low : low + chan, 0:chan]
+    conv_grad_out[2, 1, 0 : half - chan] = full[low + chan : low + half, 0:chan]
+    conv_grad_out[2, 1, half - chan :] = full[low : low + 2 * chan - half, chan : 2 * chan]
+    conv_grad_out[2, 2] = full[low + 2 * chan - half : low + half, chan : 2 * chan]
     bias_out[...] = sum(full[rows + 8 * t : rows + 8 * t + 1, 0:chan] for t in range(3))
     grad_copy = pltpu.make_async_copy(conv_grad_out, conv_grad_hbm, sem.at[1])
     bias_copy = pltpu.make_async_copy(bias_out, bias_hbm, sem.at[2])
@@ -555,14 +746,18 @@
                 pltpu.VMEM((2, n_row, 8, rank), F32),
                 pltpu.VMEM((edge + 16, rank), F32),
                 pltpu.VMEM((edge + 16, rank), F32),
-                pltpu.VMEM((3 * edge, rank), BF16),
+                pltpu.VMEM((pairs + 8, 2 * rank), F32),
+                pltpu.VMEM((256, 256), BF16),
+                pltpu.VMEM((3, 2 * edge, 2 * edge), BF16),
+                pltpu.VMEM((3 * chan, 4 * chan), BF16),
                 pltpu.VMEM((chan, edge, edge), BF16),
                 pltpu.VMEM((chan * edge, edge), F32),
-                pltpu.VMEM(((pairs + 2) * 3 * chan, 2 * edge), BF16),
-                pltpu.VMEM(((pairs + 4) * chan, 2 * edge), F32),
-                pltpu.VMEM(((pairs + 4) * chan, 2 * edge), BF16),
+                pltpu.VMEM((pairs * chan, 2 * edge), BF16),
+                pltpu.VMEM((16 * 3 * chan, 2 * edge), BF16),
+                pltpu.VMEM((16 * chan, 2 * edge), F32),
+                pltpu.VMEM((16 * chan, 2 * edge), BF16),
                 pltpu.VMEM((3 * chan, 3 * chan), F32),
-                pltpu.VMEM((3 * chan, 3 * chan), F32),
+                pltpu.VMEM((3 * chan, 4 * chan), F32),
                 pltpu.VMEM((chan, 2 * edge), F32),
                 pltpu.VMEM((n_own * chunk, 128), F32),
                 pltpu.VMEM((n_all, chunk, 128), F32),

time: 35.1 us -> 30.5 us (0.87)
  Pallas kernels: 33.7 us -> 29.1 us
    pallas_call x1, Pallas kernels: 32.8 us -> 28.2 us  [per_device(): pl.pallas_call(functools.partial(kernel, (n_row, n_col, n_rep, edge, chan...]
where the time goes in v2:
time: 30.5 us; the launch traced here: 30.4 us
  Pallas kernels  29.1 us (95%)
  between operations  1.29 us (4%)
    pallas_call x1, Pallas kernels, per_device(): pl.pallas_call(functools.partial(kernel, (n_row, n_col, n_rep, edge, chan...  28.2 us
    pallas_call x1, Pallas kernels, per_device(): pl.pallas_call(finish, out_shape=(jax.ShapeDtypeStruct((edge, edge), F32)...  0.83 us

profile of v2, /device:TPU:0, one launch (start us, length us, event | category | flops | bytes accessed | tf_op | source)
XLA Modules:
  0.0 30.4 jit_solution(16317820396001195127)
XLA Ops:
  1.3 28.2 %pair_step.1 = (f32[128,128]{1,0:T(8,128)S(1)}, bf16[8,40,128]{2,1,0:T(8,128)(2,1)S(1)}) custom-call(bf16[128,640]{1,0:T(8,128)(2,1)} %emb_row_hbm.1, bf16[320,128]{1,0:T(8,128)(2,1)} %bitcast.8, bf16[64,1280]{1,0:T(8,128)(2,1)} %bitcast.6, bf16[64,1280]{1,0:T(8,128)(2,1)} %bitcast.7, bf16[64,64]{1,0:T(8,128)(2,1)} %pair_out_hbm.1, f32[1,64]{1,0:T(1,128)} %bitcast.9, ...), custom_call_target="tpu_custom_call" | custom-call | tf_op jit(solution)/shard_map/pair_step/pallas_call | solution.py:721
  29.5 0.8 %finish.1 = (f32[128,128]{1,0:T(8,128)}, f32[3,3,64,64]{3,2,1,0:T(8,128)}, f32[1,64]{1,0:T(1,128)}) custom-call(f32[128,128]{1,0:T(8,128)S(1)} %get-tuple-element.8.loss, bf16[8,40,128]{2,1,0:T(8,128)(2,1)S(1)} %get-tuple-element.9.gathered), custom_call_target="tpu_custom_call" | custom-call | tf_op jit(solution)/shard_map/finish/pallas_call | solution.py:781

commit v3 on v2

--- a/solution.py
+++ b/solution.py
@@ -72,6 +72,7 @@
     kept,
     loss_out,
     full,
+    full_side,
     emb_row,
     emb_col,
     proj_row,
@@ -94,7 +95,6 @@
     wide,
     weight_t,
     target_in,
-    target32,
     aims,
     hid,
     base,
@@ -102,9 +102,11 @@
     weight_f,
     total,
     bias_acc,
+    spill,
     part,
     reduced,
-    whole,
+    own_side,
+    sides,
     target_sem,
     row_send,
     row_recv,
@@ -118,6 +120,10 @@
     rs_recv,
     ag_send,
     ag_recv,
+    side_send,
+    side_recv,
+    full_send,
+    full_recv,
 ):
     n_row, n_col, n_rep, edge, chan, n_own, first_own, chunk = sizes
     n_all = n_row * n_col * n_rep
@@ -195,14 +201,18 @@
     colbuf[row] = part_col.astype(BF16)
     rowbuf[col, 0:rank, :] = part_row.astype(BF16)
     rowbuf[col, rank:, :] = jnp.full((16, edge), keep, F32).astype(BF16)
+    ends = ((edge - 2, edge - 1), (0, 1))
+
+    def pair_row(values, at):
+        return jnp.concatenate([values[r : r + 1] for r in at], axis=1)
+
     turned = rounded(part_col).T
-    coltail[0] = turned[edge - 8 :]
-    coltail[1] = turned[0:8]
+    for side in range(2):
+        coltail[side] = pair_row(turned, ends[side])
     turned = rounded(part_row).T
-    rowtail[0, 0:8] = turned[edge - 8 :]
-    rowtail[1, 0:8] = turned[0:8]
     for side in range(2):
-        rowtail[side, 8:16] = jnp.full((8, rank), keep, F32)
+        rowtail[side, 0:1] = pair_row(turned, ends[side])
+        rowtail[side, 1:2] = jnp.full((1, 2 * rank), keep, F32)
 
     pl.semaphore_wait(barrier, n_all - 1)
 
@@ -231,13 +241,16 @@
             device_id_type=MESH,
         )
 
-    def col_copy(d, src):
+    def col_copy(k, src):
+        down, up = n_row - 1 - k, k
+        down = down - (down <= row).astype(jnp.int32)
+        up = up + (up >= row).astype(jnp.int32)
         return pltpu.make_async_remote_copy(
             src_ref=colbuf.at[src],
             dst_ref=colbuf.at[src],
             send_sem=col_send,
             recv_sem=col_recv,
-            device_id={"row": lax.rem(row + d, n_row)},
+            device_id={"row": jnp.where(2 * row < n_row, down, up)},
             device_id_type=MESH,
         )
 
@@ -254,7 +267,7 @@
 
     for side in range(2):
         loop(0, n_row, lambda d: cedge_copy(side, d, row).start())
-    loop(1, n_row, lambda d: col_copy(d, row).start())
+    loop(0, n_row - 1, lambda k: col_copy(k, row).start())
     for side in range(2):
         loop(0, n_col, lambda d: redge_copy(side, d, col).start())
     loop(1, n_col, lambda d: row_copy(d, col).start())
@@ -271,20 +284,17 @@
     for copy in inputs[4:]:
         copy.wait()
 
-    def widen(c, _):
-        start = pl.multiple_of(c * edge, edge)
-        target32[pl.ds(start, edge), :] = target_in[c].astype(F32)
+    def lay(i, _):
+        for low in range(0, chan, 16):
+            block = target_in[low : low + 16, pl.ds(pl.multiple_of(i * 16, 16), 16), :]
+            block = jnp.swapaxes(block.astype(F32), 0, 1)
+            for r in range(16):
+                start = pl.multiple_of((i * 8 + r // 2) * chan + low, 16)
+                lanes = slice(r % 2 * edge, (r % 2 + 1) * edge)
+                aims[pl.ds(start, 16), lanes] = block[r].astype(BF16)
         return 0
 
-    lax.fori_loop(0, chan, widen, 0, unroll=4)
-    def lay(p, _):
-        for r in range(2):
-            aim = target32[pl.ds(2 * p + r, chan, stride=edge), :].astype(BF16)
-            start = pl.multiple_of(p * chan, chan)
-            aims[pl.ds(start, chan), r * edge : (r + 1) * edge] = aim
-        return 0
-
-    lax.fori_loop(0, pairs, lay, 0, unroll=2)
+    lax.fori_loop(0, edge // 16, lay, 0)
     for a in range(3):
         for b in range(3):
             weight_f[b * chan : (b + 1) * chan, a * chan : (a + 1) * chan] = conv_weight[
@@ -316,12 +326,16 @@
     def summed(terms):
         return sum(x.astype(F32) for x in terms)
 
-    row_feat[0:8, :] = rounded(summed(rowedge[0, c, 0:8, :] for c in range(n_col)))
+    def unpack(target, values, low):
+        for r in range(2):
+            target[low + r : low + r + 1, :] = values[:, r * rank : (r + 1) * rank]
+
+    for side, low in ((0, 6), (1, edge + 8)):
+        edge_sum = rounded(summed(rowedge[side, c, 0:1, :] for c in range(n_col)))
+        unpack(row_feat, edge_sum, low)
+        unpack(col_wide, summed(coledge[side, r] for r in range(n_row)), low)
     row_feat[8 : edge + 8, :] = rounded(summed(rowbuf[c, 0:rank, :] for c in range(n_col))).T
-    row_feat[edge + 8 :, :] = rounded(summed(rowedge[1, c, 0:8, :] for c in range(n_col)))
-    col_wide[0:8, :] = summed(coledge[0, r] for r in range(n_row))
     col_wide[8 : edge + 8, :] = summed(colbuf[r] for r in range(n_row)).T
-    col_wide[edge + 8 :, :] = summed(coledge[1, r] for r in range(n_row))
     feat_pairs[0 : pairs + 2, :] = jnp.concatenate(
         [row_feat[pl.ds(6 + r, pairs + 2, stride=2), :] for r in range(2)], axis=1
     )
@@ -338,9 +352,9 @@
         )
         return (jnp.where(lane < 2, left, here), here, jnp.where(lane >= edge - 2, right, here))
 
-    top = masks(lambda c: rowedge[0, c, 8:9, 0:1], (line > 0).astype(F32))
+    top = masks(lambda c: rowedge[0, c, 1:2, 0:1], (line > 0).astype(F32))
     middle = masks(lambda c: rowbuf[c, rank:, 0:1].astype(F32)[0:1], jnp.float32(1))
-    bottom = masks(lambda c: rowedge[1, c, 8:9, 0:1], (line < n_line - 1).astype(F32))
+    bottom = masks(lambda c: rowedge[1, c, 1:2, 0:1], (line < n_line - 1).astype(F32))
 
     shifted = [col_wide[6 + 2 * b : 6 + 2 * b + edge, :].T for b in range(3)]
     first_rows = lax.broadcasted_iota(jnp.int32, (2 * edge - 2 * rank, 2 * edge), 0) < 3
@@ -471,7 +485,7 @@
                 pltpu.matmul_acc_lhs(spares[unit], left, load_staged_rhs=at)
 
             def after():
-                part[0:16, :] = pltpu.matmul_pop(spares[unit])[:, 0:128]
+                spill[...] = pltpu.matmul_pop(spares[unit])[:, 0:128]
 
             return push_wide(unit, b), go, after, 1
 
@@ -586,86 +600,107 @@
     )
     bias_sum = (bias_acc[:, 0:edge] + bias_acc[:, edge:]).T
     bias_sum = jnp.sum(bias_sum, axis=0, keepdims=True) * norm
-    bias_sum = jnp.broadcast_to(bias_sum, (8, chan))
-    part[0:rows, :] = flat
-    for term in range(3):
-        low = rows + 8 * term
-        part[low : low + 8, :] = jnp.concatenate([bias_sum, bias_sum], axis=1)
-    rest = n_own * chunk - rows - 24
-    if rest > 0:
-        part[rows + 24 :, :] = jnp.zeros((rest, 128), F32)
+
+    def coded(values, most):
+        most = jnp.maximum(most, 1e-33)
+        return jnp.round(values * (32767.0 / most)).astype(jnp.int32), most / 32767.0
+
+    def largest(values):
+        return jnp.max(jnp.max(jnp.abs(values), axis=0, keepdims=True), axis=1, keepdims=True)
+
+    def side_row(bias, scale):
+        return jnp.concatenate([bias, jnp.broadcast_to(scale, (1, 128 - chan))], axis=1)
+
+    codes, scale = coded(flat, largest(flat))
+    for index in range(n_own):
+        have = min(max(rows - index * chunk, 0), chunk)
+        values = [codes[index * chunk : index * chunk + have]] if have else []
+        if have < chunk:
+            values.append(jnp.zeros((chunk - have, 128), jnp.int32))
+        values = jnp.concatenate(values, axis=0)
+        part[index] = values.astype(jnp.int16)
+    own_side[...] = side_row(bias_sum, scale)
 
     mine = me - first_own
     owner = (mine >= 0) & (mine < n_own)
 
-    def piece(index):
-        return pl.ds(pl.multiple_of(index * chunk, 8), chunk)
+    def remote(src, dst, send_sem, recv_sem, to):
+        return pltpu.make_async_remote_copy(
+            src_ref=src,
+            dst_ref=dst,
+            send_sem=send_sem,
+            recv_sem=recv_sem,
+            device_id=to,
+            device_id_type=MESH,
+        )
 
     def scatter(d):
         index = lax.rem(me + d, n_own)
 
         @pl.when(first_own + index != me)
         def _():
-            pltpu.make_async_remote_copy(
-                src_ref=part.at[piece(index)],
-                dst_ref=reduced.at[me],
-                send_sem=rs_send,
-                recv_sem=rs_recv,
-                device_id=device(first_own + index),
-                device_id_type=MESH,
-            ).start()
+            to = device(first_own + index)
+            remote(own_side, sides.at[me], side_send, side_recv, to).start()
+            remote(part.at[index], reduced.at[me], rs_send, rs_recv, to).start()
 
     def gather(d):
-        pltpu.make_async_remote_copy(
-            src_ref=full.at[mine],
-            dst_ref=full.at[mine],
-            send_sem=ag_send,
-            recv_sem=ag_recv,
-            device_id=device(lax.rem(me + d, n_all)),
-            device_id_type=MESH,
-        ).start()
+        to = device(lax.rem(me + d, n_all))
+        remote(full_side.at[mine], full_side.at[mine], full_send, full_recv, to).start()
+        remote(full.at[mine], full.at[mine], ag_send, ag_recv, to).start()
 
     loop(0, n_own, scatter)
 
     @pl.when(owner)
     def _():
-        reduced[me] = part[piece(mine), :]
+        reduced[me] = part[mine]
+        sides[me] = own_side[...]
+        await_bytes(sides.at[0 : n_all - 1], side_recv)
         await_bytes(reduced.at[0 : n_all - 1], rs_recv)
+
+        def decoded(r):
+            return reduced[r].astype(jnp.int32).astype(F32) * sides[r][:, 127:128]
+
         if n_all <= 16:
-            own = sum(reduced[r] for r in range(n_all))
+            own = sum(decoded(r) for r in range(n_all))
+            bias = sum(sides[r] for r in range(n_all))
         else:
             own = lax.fori_loop(
-                0, n_all, lambda r, x: x + reduced[r], jnp.zeros((chunk, 128), F32)
+                0, n_all, lambda r, x: x + decoded(r), jnp.zeros((chunk, 128), F32)
             )
-        at = mine * chunk + lax.broadcasted_iota(jnp.int32, (chunk, 128), 0)
-        second = own - rounded(own)
-        third = second - rounded(second)
-        own = jnp.where(at >= rows + 8, jnp.where(at >= rows + 16, third, second), own)
-        full[mine] = own.astype(BF16)
+            bias = lax.fori_loop(0, n_all, lambda r, x: x + sides[r], jnp.zeros((1, 128), F32))
+        codes, scale = coded(own, largest(own))
+        full[mine] = codes.astype(jnp.int16)
+        full_side[mine] = side_row(bias[:, 0:chan], scale)
         loop(1, n_all, gather)
         if n_own > 1:
+            await_bytes(full_side.at[0 : n_own - 1], full_recv)
             await_bytes(full.at[0 : n_own - 1], ag_recv)
-            await_bytes(part.at[0 : (n_own - 1) * chunk], rs_send)
+            await_bytes(sides.at[0 : n_own - 1], side_send)
+            await_bytes(part.at[0 : n_own - 1], rs_send)
 
     @pl.when(jnp.logical_not(owner))
     def _():
+        await_bytes(full_side, full_recv)
         await_bytes(full, ag_recv)
+        await_bytes(sides.at[0:n_own], side_send)
         await_bytes(part, rs_send)
 
     await_features(col_send, row_send, cedge_send, redge_send)
 
     @pl.when(owner)
     def _():
-        await_bytes(whole, ag_send)
-
-
-def finish(loss, gathered, loss_hbm, conv_grad_hbm, bias_hbm, full, conv_grad_out, bias_out, sem):
+        await_bytes(sides.at[0 : n_all - 1], full_send)
+        await_bytes(reduced.at[0 : n_all - 1], ag_send)
+
+
+def finish(loss, gathered, side, loss_hbm, conv_grad_hbm, bias_hbm, full, conv_grad_out, bias_out, sem):
     n_all, chunk = gathered.shape[0:2]
     loss_copy = pltpu.make_async_copy(loss, loss_hbm, sem.at[0])
     loss_copy.start()
 
     def place(r):
-        full[pl.ds(r * chunk, chunk), :] = gathered[r].astype(F32)
+        value = gathered[r].astype(jnp.int32).astype(F32) * side[r][:, 127:128]
+        full[pl.ds(r * chunk, chunk), :] = value
 
     loop(0, n_all, place)
     chan = bias_out.shape[1]
@@ -680,7 +715,7 @@
     conv_grad_out[2, 1, 0 : half - chan] = full[low + chan : low + half, 0:chan]
     conv_grad_out[2, 1, half - chan :] = full[low : low + 2 * chan - half, chan : 2 * chan]
     conv_grad_out[2, 2] = full[low + 2 * chan - half : low + half, chan : 2 * chan]
-    bias_out[...] = sum(full[rows + 8 * t : rows + 8 * t + 1, 0:chan] for t in range(3))
+    bias_out[...] = side[0][:, 0:chan]
     grad_copy = pltpu.make_async_copy(conv_grad_out, conv_grad_hbm, sem.at[1])
     bias_copy = pltpu.make_async_copy(bias_out, bias_hbm, sem.at[2])
     grad_copy.start()
@@ -709,7 +744,7 @@
         chan, edge = target.shape[0], target.shape[1]
         rank = pair_out.shape[0]
         pairs = edge // 2
-        used = 3 * chan + 3 * chan // 2 + 24
+        used = 3 * chan + 3 * chan // 2
         inner = n_row // 2 if n_row >= 4 else n_row
         n_own = inner * n_col * n_rep
         first_own = (n_row - inner) // 2 * n_col * n_rep
@@ -718,16 +753,17 @@
         dma = pltpu.SemaphoreType.DMA
         vmem = pl.BlockSpec(memory_space=pltpu.VMEM)
         hbm = pl.BlockSpec(memory_space=pltpu.HBM)
-        loss, sums = pl.pallas_call(
+        results = pl.pallas_call(
             functools.partial(
                 kernel, (n_row, n_col, n_rep, edge, chan, n_own, first_own, chunk)
             ),
             out_shape=(
                 pltpu.VMEM((edge, edge), F32),
-                pltpu.VMEM((n_own, chunk, 128), BF16),
+                pltpu.VMEM((n_own, chunk, 128), jnp.int16),
+                pltpu.VMEM((n_own, 1, 128), F32),
             ),
             in_specs=[hbm] * 9 + [pl.BlockSpec(memory_space=pltpu.SMEM)],
-            out_specs=(vmem,) * 2,
+            out_specs=(vmem,) * 3,
             scratch_shapes=[
                 pltpu.VMEM(emb_row.shape, BF16),
                 pltpu.VMEM(emb_col.shape[::-1], BF16),
@@ -738,12 +774,12 @@
                 pltpu.VMEM((1, chan), F32),
                 pltpu.VMEM((1, chan), F32),
                 dma((8,)),
-                pltpu.VMEM((2, 16, rank), F32),
-                pltpu.VMEM((2, 8, rank), F32),
+                pltpu.VMEM((2, 2, 2 * rank), F32),
+                pltpu.VMEM((2, 1, 2 * rank), F32),
                 pltpu.VMEM((n_col, rank + 16, edge), BF16),
-                pltpu.VMEM((2, n_col, 16, rank), F32),
+                pltpu.VMEM((2, n_col, 2, 2 * rank), F32),
                 pltpu.VMEM((n_row, rank, edge), BF16),
-                pltpu.VMEM((2, n_row, 8, rank), F32),
+                pltpu.VMEM((2, n_row, 1, 2 * rank), F32),
                 pltpu.VMEM((edge + 16, rank), F32),
                 pltpu.VMEM((edge + 16, rank), F32),
                 pltpu.VMEM((pairs + 8, 2 * rank), F32),
@@ -751,7 +787,6 @@
                 pltpu.VMEM((3, 2 * edge, 2 * edge), BF16),
                 pltpu.VMEM((3 * chan, 4 * chan), BF16),
                 pltpu.VMEM((chan, edge, edge), BF16),
-                pltpu.VMEM((chan * edge, edge), F32),
                 pltpu.VMEM((pairs * chan, 2 * edge), BF16),
                 pltpu.VMEM((16 * 3 * chan, 2 * edge), BF16),
                 pltpu.VMEM((16 * chan, 2 * edge), F32),
@@ -759,10 +794,12 @@
                 pltpu.VMEM((3 * chan, 3 * chan), F32),
                 pltpu.VMEM((3 * chan, 4 * chan), F32),
                 pltpu.VMEM((chan, 2 * edge), F32),
-                pltpu.VMEM((n_own * chunk, 128), F32),
-                pltpu.VMEM((n_all, chunk, 128), F32),
-                pltpu.VMEM((n_all - 1, chunk, 128), BF16),
-                *[pltpu.SemaphoreType.DMA] * 13,
+                pltpu.VMEM((16, 128), F32),
+                pltpu.VMEM((n_own, chunk, 128), jnp.int16),
+                pltpu.VMEM((n_all, chunk, 128), jnp.int16),
+                pltpu.VMEM((1, 128), F32),
+                pltpu.VMEM((n_all, 1, 128), F32),
+                *[pltpu.SemaphoreType.DMA] * 17,
             ],
             compiler_params=pltpu.CompilerParams(collective_id=0, has_side_effects=True),
             name="pair_step",
@@ -785,7 +822,7 @@
                 jax.ShapeDtypeStruct((3, 3, chan, chan), F32),
                 jax.ShapeDtypeStruct((1, chan), F32),
             ),
-            in_specs=[vmem] * 2,
+            in_specs=[vmem] * 3,
             out_specs=(hbm,) * 3,
             scratch_shapes=[
                 pltpu.VMEM((n_own * chunk, 128), F32),
@@ -795,7 +832,7 @@
             ],
             name="finish",
         )(
-            *(pltpu.with_memory_space_constraint(x, pltpu.VMEM) for x in (loss, sums))
+            *(pltpu.with_memory_space_constraint(x, pltpu.VMEM) for x in results)
         )
         return loss, grads, bias.reshape(chan)
 

time: 30.5 us -> 28.5 us (0.934)
  Pallas kernels: 29.1 us -> 27.1 us
    pallas_call x1, Pallas kernels: 28.2 us -> 26.2 us  [per_device(): pl.pallas_call(functools.partial(kernel, (n_row, n_col, n_rep, edge, chan...]
where the time goes in v3:
time: 28.5 us; the launch traced here: 28.4 us
  Pallas kernels  27.1 us (95%)
  between operations  1.29 us (5%)
    pallas_call x1, Pallas kernels, per_device(): pl.pallas_call(functools.partial(kernel, (n_row, n_col, n_rep, edge, chan...  26.2 us
    pallas_call x1, Pallas kernels, per_device(): pl.pallas_call(finish, out_shape=(jax.ShapeDtypeStruct((edge, edge), F32)...  0.92 us

profile of v3, /device:TPU:0, one launch (start us, length us, event | category | flops | bytes accessed | tf_op | source)
XLA Modules:
  0.0 28.4 jit_solution(10219354481021965926)
XLA Ops:
  1.3 26.2 %pair_step.1 = (f32[128,128]{1,0:T(8,128)S(1)}, s16[8,40,128]{2,1,0:T(8,128)(2,1)S(1)}, f32[8,1,128]{2,1,0:T(1,128)S(1)}) custom-call(bf16[128,640]{1,0:T(8,128)(2,1)} %emb_row_hbm.1, bf16[320,128]{1,0:T(8,128)(2,1)} %bitcast.8, bf16[64,1280]{1,0:T(8,128)(2,1)} %bitcast.6, bf16[64,1280]{1,0:T(8,128)(2,1)} %bitcast.7, bf16[64,64]{1,0:T(8,128)(2,1)} %pair_out_hbm.1, ...), custom_call_target="tpu_custom_call" | custom-call | tf_op jit(solution)/shard_map/pair_step/pallas_call | solution.py:756
  27.4 0.9 %finish.1 = (f32[128,128]{1,0:T(8,128)}, f32[3,3,64,64]{3,2,1,0:T(8,128)}, f32[1,64]{1,0:T(1,128)}) custom-call(f32[128,128]{1,0:T(8,128)S(1)} %get-tuple-element.9.loss, s16[8,40,128]{2,1,0:T(8,128)(2,1)S(1)} %get-tuple-element.10.gathered, f32[8,1,128]{2,1,0:T(1,128)S(1)} %get-tuple-element.11.side), custom_call_target="tpu_custom_call" | custom-call | tf_op jit(solution)/shard_map/finish/pallas_call | solution.py:818

commit v4 on v3

--- a/solution.py
+++ b/solution.py
@@ -21,18 +21,22 @@
         lax.fori_loop(low, high, lambda d, _: (body(d), 0)[1], 0)
 
 
-def columns(ref, width, index, count):
-    everything = ref.shape[1]
+def window_of(everything, width, index, count):
     if width % 128 == 0:
-        return ref[:, pl.ds(pl.multiple_of(index * width, 128), width)]
+        return index * width, width, 0
     offset = max(i * width % 128 for i in range(count))
     window = min(-(-(offset + width) // 128) * 128, everything)
-    tile = index * width // 128
+    tile = lax.div(index * width, 128)
     if any(i * width // 128 * 128 + window > everything for i in range(count)):
         tile = jnp.minimum(tile, (everything - window) // 128)
-    value = ref[:, pl.ds(pl.multiple_of(tile * 128, 128), window)].astype(F32)
-    shift = window - (index * width - tile * 128)
-    value = pltpu.roll(value, lax.rem(shift, window), 1)
+    return tile * 128, window, index * width - tile * 128
+
+
+def columns(ref, width, shift):
+    window = ref.shape[1]
+    if width % 128 == 0:
+        return ref[...]
+    value = pltpu.roll(ref[...].astype(F32), lax.rem(window - shift, window), 1)
     lane = lax.broadcasted_iota(jnp.int32, value.shape, 1)
     return jnp.where(lane < width, value, 0.0).astype(BF16)
 
@@ -102,7 +106,6 @@
     weight_f,
     total,
     bias_acc,
-    spill,
     part,
     reduced,
     own_side,
@@ -138,26 +141,34 @@
         along = lax.div(index, n_col)
         return {"row": lax.div(along, n_rep), "rep": lax.rem(along, n_rep), "col": across}
 
+    def wrapped(index, count):
+        return jnp.where(index >= count, index - count, index)
+
+    def far(k):
+        down, up = n_row - 1 - k, k
+        down = down - (down <= row).astype(jnp.int32)
+        up = up + (up >= row).astype(jnp.int32)
+        return jnp.where(2 * row < n_row, down, up)
+
     def await_bytes(ref, sem):
         pltpu.make_async_copy(ref, ref, sem).wait()
 
-    barrier = pltpu.get_barrier_semaphore()
-    loop(
-        1,
-        n_all,
-        lambda d: pl.semaphore_signal(
-            barrier, inc=1, device_id=device(lax.rem(me + d, n_all)), device_id_type=MESH
-        ),
-    )
+    col_width, row_width = emb_col.shape[0], emb_row.shape[1]
+    everything = proj_col_hbm.shape[1]
+    col_low, col_window, col_shift = window_of(everything, col_width, row, n_row)
+    row_low, row_window, row_shift = window_of(everything, row_width, col, n_col)
+
+    def lanes(low, window):
+        return pl.ds(pl.multiple_of(low, 128), window)
 
     inputs = [
         pltpu.make_async_copy(src, dst, in_sem.at[i])
         for i, (src, dst) in enumerate(
             (
+                (emb_col_hbm, emb_col),
+                (proj_col_hbm.at[:, lanes(col_low, col_window)], proj_col),
                 (emb_row_hbm, emb_row),
-                (proj_row_hbm, proj_row),
-                (emb_col_hbm, emb_col),
-                (proj_col_hbm, proj_col),
+                (proj_row_hbm.at[:, lanes(row_low, row_window)], proj_row),
                 (conv_weight_hbm, conv_weight),
                 (pair_out_hbm, pair_out),
                 (pair_bias_hbm, pair_bias),
@@ -167,54 +178,36 @@
     ]
     for copy in inputs:
         copy.start()
-    fetch = pltpu.make_async_copy(target, target_in, target_sem)
-    fetch.start()
+    barrier = pltpu.get_barrier_semaphore()
+
+    def greet(to):
+        pl.semaphore_signal(barrier, inc=1, device_id=to, device_id_type=MESH)
+
+    if n_all <= 16:
+        for k in range(n_row):
+            for c in range(n_col - 1, -1, -1):
+                for r in range(n_rep - 1, -1, -1):
+                    if k < n_row - 1 or c + r > 0:
+                        greet(
+                            {
+                                "row": far(k) if k < n_row - 1 else row,
+                                "col": wrapped(col + c, n_col),
+                                "rep": wrapped(rep + r, n_rep),
+                            }
+                        )
+    else:
+        loop(1, n_all, lambda d: greet(device(lax.rem(me + d, n_all))))
+
 
     def rounded(x):
         return x.astype(BF16).astype(F32)
 
-    for copy in inputs[2:4]:
-        copy.wait()
     rank = proj_row.shape[0]
-
-    def project(col_sum, row_sum):
-        width = emb_col.shape[0]
-        left = columns(proj_col, width, row, n_row)
-        for low in range(0, width, 256):
-            right = padded(emb_col[low : min(low + 256, width), :], square)
-            pltpu.matmul_push_rhs(right, 0, 0)
-            pltpu.matmul_acc_lhs(col_sum, wide_tile(left, low), load_staged_rhs=0)
-        for copy in inputs[0:2]:
-            copy.wait()
-        width = emb_row.shape[1]
-        left = columns(proj_row, width, col, n_col)
-        for low in range(0, width, 256):
-            right = padded(emb_row[:, low : min(low + 256, width)], square)
-            pltpu.matmul_push_rhs(right, 0, 1, transpose=True)
-            pltpu.matmul_acc_lhs(row_sum, wide_tile(left, low), load_staged_rhs=0)
-        return pltpu.matmul_pop(col_sum)[:, 0:edge], pltpu.matmul_pop(row_sum)[:, 0:edge]
-
-    part_col, part_row = pl.run_scoped(
-        project, *[pltpu.ACC(unit)((rank, 256), F32) for unit in range(2)]
-    )
-    keep = kept[0, 0].astype(F32)
-    colbuf[row] = part_col.astype(BF16)
-    rowbuf[col, 0:rank, :] = part_row.astype(BF16)
-    rowbuf[col, rank:, :] = jnp.full((16, edge), keep, F32).astype(BF16)
     ends = ((edge - 2, edge - 1), (0, 1))
+    fetch = pltpu.make_async_copy(target, target_in, target_sem)
 
     def pair_row(values, at):
         return jnp.concatenate([values[r : r + 1] for r in at], axis=1)
-
-    turned = rounded(part_col).T
-    for side in range(2):
-        coltail[side] = pair_row(turned, ends[side])
-    turned = rounded(part_row).T
-    for side in range(2):
-        rowtail[side, 0:1] = pair_row(turned, ends[side])
-        rowtail[side, 1:2] = jnp.full((1, 2 * rank), keep, F32)
-
-    pl.semaphore_wait(barrier, n_all - 1)
 
     def row_copy(d, src):
         return pltpu.make_async_remote_copy(
@@ -242,15 +235,12 @@
         )
 
     def col_copy(k, src):
-        down, up = n_row - 1 - k, k
-        down = down - (down <= row).astype(jnp.int32)
-        up = up + (up >= row).astype(jnp.int32)
         return pltpu.make_async_remote_copy(
             src_ref=colbuf.at[src],
             dst_ref=colbuf.at[src],
             send_sem=col_send,
             recv_sem=col_recv,
-            device_id={"row": jnp.where(2 * row < n_row, down, up)},
+            device_id={"row": far(k)},
             device_id_type=MESH,
         )
 
@@ -265,12 +255,49 @@
             device_id_type=MESH,
         )
 
+    for copy in inputs[0:2]:
+        copy.wait()
+    fetch.start()
+
+    def project_col(col_sum):
+        left = columns(proj_col, col_width, col_shift)
+        for low in range(0, col_width, 256):
+            right = padded(emb_col[low : min(low + 256, col_width), :], square)
+            pltpu.matmul_push_rhs(right, 0, 0)
+            pltpu.matmul_acc_lhs(col_sum, wide_tile(left, low), load_staged_rhs=0)
+        return pltpu.matmul_pop(col_sum)[:, 0:edge]
+
+    def project_row(row_sum):
+        left = columns(proj_row, row_width, row_shift)
+        for low in range(0, row_width, 256):
+            right = padded(emb_row[:, low : min(low + 256, row_width)], square)
+            pltpu.matmul_push_rhs(right, 0, 1, transpose=True)
+            pltpu.matmul_acc_lhs(row_sum, wide_tile(left, low), load_staged_rhs=0)
+        return pltpu.matmul_pop(row_sum)[:, 0:edge]
+
+    part_col = pl.run_scoped(project_col, pltpu.ACC(0)((rank, 256), F32))
+    colbuf[row] = part_col.astype(BF16)
+    pl.semaphore_wait(barrier, n_all - 1)
+    loop(0, n_row - 1, lambda k: col_copy(k, row).start())
+    turned = rounded(part_col).T
+    for side in range(2):
+        coltail[side] = pair_row(turned, ends[side])
     for side in range(2):
         loop(0, n_row, lambda d: cedge_copy(side, d, row).start())
-    loop(0, n_row - 1, lambda k: col_copy(k, row).start())
+
+    for copy in inputs[2:4]:
+        copy.wait()
+    part_row = pl.run_scoped(project_row, pltpu.ACC(1)((rank, 256), F32))
+    keep = kept[0, 0].astype(F32)
+    rowbuf[col, 0:rank, :] = part_row.astype(BF16)
+    rowbuf[col, rank:, :] = jnp.full((16, edge), keep, F32).astype(BF16)
+    loop(1, n_col, lambda d: row_copy(d, col).start())
+    turned = rounded(part_row).T
+    for side in range(2):
+        rowtail[side, 0:1] = pair_row(turned, ends[side])
+        rowtail[side, 1:2] = jnp.full((1, 2 * rank), keep, F32)
     for side in range(2):
         loop(0, n_col, lambda d: redge_copy(side, d, col).start())
-    loop(1, n_col, lambda d: row_copy(d, col).start())
 
     def await_features(col_sem, row_sem, cedge_sem, redge_sem):
         await_bytes(coledge, cedge_sem)
@@ -399,18 +426,9 @@
         loss_out[pl.ds(at, 1), :] = loss[:, 0:edge]
         loss_out[pl.ds(at + 1, 1), :] = loss[:, edge : 2 * edge]
 
-    def main(sum0, sum1, sum2, sum3, left0, left1, mid0, mid1, spare0, grad0, right0, right1, spare1, halo, grad1):
-        sums, lefts, mids, rights = (
-            (sum0, sum1, sum2, sum3),
-            (left0, left1),
-            (mid0, mid1),
-            (right0, right1),
-        )
-        spares, grads = (spare0, spare1), (grad0, grad1)
-        stage = [0, 0]
-
-        def push_wide(unit, b):
-            return lambda at: pltpu.matmul_push_rhs(wide[b], at, unit)
+    def main(*accs):
+        sums, grads, halo, features_of = accs[0:4], accs[4:6], accs[6], (accs[7:10], accs[10:16])
+        stage, primed = [0, 0], [False, False]
 
         def halo_item(p, offset, b, mask):
             def push(at):
@@ -424,6 +442,9 @@
             return push, go, None, 4
 
         def feature_item(unit, b, p, offset, acc, memo):
+            def push(at):
+                pltpu.matmul_push_rhs(wide[b], at, unit)
+
             def go(at):
                 if offset not in memo:
                     memo[offset] = scaled(p + offset, 2)
@@ -437,7 +458,7 @@
                     if b == 1:
                         base[slot(offset + r), :] = own + conv_b
 
-            return push_wide(unit, b), go, after, 8
+            return push, go, after, 8
 
         def conv_item(p, offset):
             taps = [a for a in range(3) if inside(p, offset + 1 - a)]
@@ -479,76 +500,80 @@
 
             return push, go, None, 12
 
-        def spare_item(unit, b):
-            def go(at):
-                left = jnp.zeros((16, 2 * edge), BF16)
-                pltpu.matmul_acc_lhs(spares[unit], left, load_staged_rhs=at)
-
-            def after():
-                spill[...] = pltpu.matmul_pop(spares[unit])[:, 0:128]
-
-            return push_wide(unit, b), go, after, 1
-
-        def run(queues, tails=(None, None), primed=True):
+        def run(queues, follow=(None, None)):
             spent, at, waiting = [0, 0], [0, 0], []
             for unit in range(2):
-                if queues[unit] and not primed:
+                if queues[unit] and not primed[unit]:
                     queues[unit][0][0](stage[unit])
+                primed[unit] = False
             while any(at[u] < len(queues[u]) for u in range(2)):
                 unit = min(
                     (u for u in range(2) if at[u] < len(queues[u])), key=lambda u: spent[u]
                 )
                 queue, index = queues[unit], at[unit]
                 _, go, after, cost = queue[index]
-                later = queue[index + 1][0] if index + 1 < len(queue) else tails[unit]
                 while len(waiting) > 1:
                     waiting.pop(0)()
                 go(stage[unit])
                 stage[unit] = 1 - stage[unit]
-                if later is not None:
-                    later(stage[unit])
+                if index + 1 < len(queue):
+                    queue[index + 1][0](stage[unit])
                 at[unit] += 1
                 spent[unit] += cost
                 if after is not None:
                     waiting.append(after)
             for after in waiting:
                 after()
-
-        tails = (push_wide(0, 0), push_wide(1, 2))
-
-        def features(p, low):
-            memo = {}
-            first, second = [], []
-            for half in range(2):
-                offset = low + 2 * half
-                first.append(feature_item(0, 0, p, offset, lefts[half], memo))
-                first.append(feature_item(0, 1, p, offset, mids[half], memo))
-                second.append(feature_item(1, 2, p, offset, rights[half], memo))
-            return first, second
-
-        def merged(own, other):
-            return own[0:2] + other[0:2] + own[2:4] + other[2:]
+            for unit in range(2):
+                if follow[unit] is not None:
+                    follow[unit][0](stage[unit])
+                    primed[unit] = True
+
+        def features(p, low, units=(1, 1)):
+            items = []
+            for half, unit in enumerate(units):
+                memo = {}
+                held = features_of[unit][3 * half * unit : 3 * half * unit + 3]
+                items.append(
+                    [
+                        feature_item(unit, b, p, low + 2 * half, held[b], memo)
+                        for b in range(3)
+                    ]
+                )
+            return items
+
+        def convs(p, low, high):
+            return [conv_item(p, r) for r in range(low, high)]
+
+        def turns(unit, p, *offsets):
+            return [grad_item(unit, p, r) for r in offsets]
 
         def group(p, low):
-            f0, f1 = features(p, low)
-            convs = [conv_item(p, low - 4 + r) for r in range(4)]
-            turns = [grad_item(1, p, low - 12 + r) for r in range(4)]
-            run((merged(f0, convs), [f1[0], *turns[0:2], f1[1], *turns[2:4]]), tails)
-
-        halos = [halo_item(0, -1, b, top) for b in range(3)]
-        f0, f1 = features(0, 0)
-        run((f0, halos + f1), tails, primed=False)
-        f0, f1 = features(0, 4)
-        convs = [conv_item(0, r) for r in range(-1, 4)]
-        run((merged(f0, convs) + [spare_item(0, 0)], f1), tails)
-        f0, f1 = features(0, 8)
-        convs = [conv_item(0, r) for r in range(4, 8)]
-        turns = [grad_item(1, 0, r) for r in (-1, 0, 1)]
-        run((merged(f0, convs), [f1[0], *turns[0:2], f1[1], turns[2], spare_item(1, 2)]), tails)
-        f0, f1 = features(0, 12)
-        convs = [conv_item(0, r) for r in range(8, 12)]
-        turns = [grad_item(1, 0, r) for r in (2, 3)]
-        run((merged(f0, convs), [f1[0], turns[0], f1[1], turns[1]]), tails)
+            early, late = features(p, low)
+            conv = convs(p, low - 4, low)
+            run(
+                (
+                    turns(0, p, low - 12) + conv[0:2] + turns(0, p, low - 10) + conv[2:4],
+                    turns(1, p, low - 11) + early + turns(1, p, low - 9) + late,
+                ),
+                [turns(u, p, low - 8 + u)[0] for u in range(2)],
+            )
+
+        early, late = features(0, 0, (1, 0))
+        first = convs(0, -1, 4)
+        second = features(0, 4)
+        run((late, [halo_item(0, -1, b, top) for b in range(3)] + early), (first[0], second[0][0]))
+        third, fourth = convs(0, 4, 8), features(0, 8)
+        run((first, second[0] + second[1]), (third[0], fourth[0][0]))
+        fifth, sixth = convs(0, 8, 12), features(0, 12)
+        run((third, fourth[0] + turns(1, 0, -1) + fourth[1]), (fifth[0], sixth[0][0]))
+        run(
+            (
+                fifth[0:2] + turns(0, 0, 0) + fifth[2:4] + turns(0, 0, 2),
+                sixth[0] + turns(1, 0, 1) + sixth[1] + turns(1, 0, 3),
+            ),
+            [turns(u, 0, 4 + u)[0] for u in range(2)],
+        )
 
         def step(t, _):
             p = pl.multiple_of(t * 16, 16)
@@ -557,18 +582,19 @@
             return 0
 
         lax.fori_loop(1, pairs // 16, step, 0)
-        halos = [halo_item(pairs, 0, b, bottom) for b in range(3)]
-        turns = [grad_item(1, pairs, r) for r in range(-12, -6)]
-        convs = [conv_item(pairs, r) for r in range(-4, 1)]
+        last = convs(pairs, -4, 1)
         run(
             (
-                [spare_item(0, 0)] + convs,
-                [spare_item(1, 2)] + halos + turns,
-            )
-        )
-        turns = [[grad_item(u, pairs, r) for r in range(-6 + u, 1, 2)] for u in range(2)]
-        run(turns, primed=False)
-        total[...] = pltpu.matmul_pop(grad0) + pltpu.matmul_pop(grad1)
+                turns(0, pairs, -12) + last[0:2] + turns(0, pairs, -10) + last[2:4],
+                turns(1, pairs, -11)
+                + [halo_item(pairs, 0, b, bottom) for b in range(3)]
+                + turns(1, pairs, -9, -8, -7),
+            ),
+            (last[4], turns(1, pairs, -6)[0]),
+        )
+        run((last[4:] + turns(0, pairs, -5, -4), turns(1, pairs, -6, -3)))
+        run((turns(0, pairs, -2, 0), turns(1, pairs, -1)))
+        total[...] = pltpu.matmul_pop(grads[0]) + pltpu.matmul_pop(grads[1])
 
     def accumulator(unit, rows_of):
         return pltpu.ACC(unit)((rows_of, 2 * edge), F32)
@@ -576,13 +602,10 @@
     pl.run_scoped(
         main,
         *[accumulator(0, chan)] * 4,
-        *[accumulator(0, 2 * chan)] * 4,
-        accumulator(0, 16),
-        accumulator(0, 3 * chan),
-        *[accumulator(1, 2 * chan)] * 2,
-        accumulator(1, 16),
+        *[accumulator(unit, 3 * chan) for unit in range(2)],
         accumulator(1, chan),
-        accumulator(1, 3 * chan),
+        *[accumulator(0, 2 * chan)] * 3,
+        *[accumulator(1, 2 * chan)] * 6,
     )
 
     norm = 1.0 / (edge * edge)
@@ -640,13 +663,13 @@
         @pl.when(first_own + index != me)
         def _():
             to = device(first_own + index)
+            remote(part.at[index], reduced.at[me], rs_send, rs_recv, to).start()
             remote(own_side, sides.at[me], side_send, side_recv, to).start()
-            remote(part.at[index], reduced.at[me], rs_send, rs_recv, to).start()
 
     def gather(d):
         to = device(lax.rem(me + d, n_all))
+        remote(full.at[mine], full.at[mine], ag_send, ag_recv, to).start()
         remote(full_side.at[mine], full_side.at[mine], full_send, full_recv, to).start()
-        remote(full.at[mine], full.at[mine], ag_send, ag_recv, to).start()
 
     loop(0, n_own, scatter)
 
@@ -750,6 +773,9 @@
         first_own = (n_row - inner) // 2 * n_col * n_rep
         chunk = 8 * pl.cdiv(used, 8 * n_own)
 
+        def window(width, count):
+            return window_of(proj_row.shape[0], width, 0, count)[1]
+
         dma = pltpu.SemaphoreType.DMA
         vmem = pl.BlockSpec(memory_space=pltpu.VMEM)
         hbm = pl.BlockSpec(memory_space=pltpu.HBM)
@@ -767,8 +793,8 @@
             scratch_shapes=[
                 pltpu.VMEM(emb_row.shape, BF16),
                 pltpu.VMEM(emb_col.shape[::-1], BF16),
-                pltpu.VMEM(proj_row.shape[::-1], BF16),
-                pltpu.VMEM(proj_col.shape[::-1], BF16),
+                pltpu.VMEM((rank, window(emb_row.shape[1], n_col)), BF16),
+                pltpu.VMEM((rank, window(emb_col.shape[1], n_row)), BF16),
                 pltpu.VMEM(conv_weight.shape, BF16),
                 pltpu.VMEM(pair_out.shape, BF16),
                 pltpu.VMEM((1, chan), F32),
@@ -794,7 +820,6 @@
                 pltpu.VMEM((3 * chan, 3 * chan), F32),
                 pltpu.VMEM((3 * chan, 4 * chan), F32),
                 pltpu.VMEM((chan, 2 * edge), F32),
-                pltpu.VMEM((16, 128), F32),
                 pltpu.VMEM((n_own, chunk, 128), jnp.int16),
                 pltpu.VMEM((n_all, chunk, 128), jnp.int16),
                 pltpu.VMEM((1, 128), F32),

time: 28.5 us -> 28.3 us (level)
  Pallas kernels: 27.1 us -> 26.8 us
where the time goes in v4:
time: 28.3 us; the launch traced here: 28.1 us
  Pallas kernels  26.8 us (95%)
  between operations  1.29 us (5%)
    pallas_call x1, Pallas kernels, per_device(): pl.pallas_call(functools.partial(kernel, (n_row, n_col, n_rep, edge, chan...  25.9 us
    pallas_call x1, Pallas kernels, per_device(): pl.pallas_call(finish, out_shape=(jax.ShapeDtypeStruct((edge, edge), F32)...  0.92 us

profile of v4, /device:TPU:0, one launch (start us, length us, event | category | flops | bytes accessed | tf_op | source)
XLA Modules:
  0.0 28.1 jit_solution(12777967808067539984)
XLA Ops:
  1.3 25.9 %pair_step.1 = (f32[128,128]{1,0:T(8,128)S(1)}, s16[8,40,128]{2,1,0:T(8,128)(2,1)S(1)}, f32[8,1,128]{2,1,0:T(1,128)S(1)}) custom-call(bf16[128,640]{1,0:T(8,128)(2,1)} %emb_row_hbm.1, bf16[320,128]{1,0:T(8,128)(2,1)} %bitcast.8, bf16[64,1280]{1,0:T(8,128)(2,1)} %bitcast.6, bf16[64,1280]{1,0:T(8,128)(2,1)} %bitcast.7, bf16[64,64]{1,0:T(8,128)(2,1)} %pair_out_hbm.1, ...), custom_call_target="tpu_custom_call" | custom-call | tf_op jit(solution)/shard_map/pair_step/pallas_call | solution.py:782
  27.2 0.9 %finish.1 = (f32[128,128]{1,0:T(8,128)}, f32[3,3,64,64]{3,2,1,0:T(8,128)}, f32[1,64]{1,0:T(1,128)}) custom-call(f32[128,128]{1,0:T(8,128)S(1)} %get-tuple-element.9.loss, s16[8,40,128]{2,1,0:T(8,128)(2,1)S(1)} %get-tuple-element.10.gathered, f32[8,1,128]{2,1,0:T(1,128)S(1)} %get-tuple-element.11.side), custom_call_target="tpu_custom_call" | custom-call | tf_op jit(solution)/shard_map/finish/pallas_call | solution.py:843

commit v5 on v4

--- a/solution.py
+++ b/solution.py
@@ -10,7 +10,8 @@
 MESH = pl.DeviceIdType.MESH
 F32 = jnp.float32
 BF16 = jnp.bfloat16
-NT = (((1,), (1,)), ((), ()))
+CODES = 32000.0
+LOG2E = 1.4426950408889634
 
 
 def loop(low, high, body):
@@ -76,7 +77,6 @@
     kept,
     loss_out,
     full,
-    full_side,
     emb_row,
     emb_col,
     proj_row,
@@ -108,8 +108,6 @@
     bias_acc,
     part,
     reduced,
-    own_side,
-    sides,
     target_sem,
     row_send,
     row_recv,
@@ -123,12 +121,8 @@
     rs_recv,
     ag_send,
     ag_recv,
-    side_send,
-    side_recv,
-    full_send,
-    full_recv,
 ):
-    n_row, n_col, n_rep, edge, chan, n_own, first_own, chunk = sizes
+    n_row, n_col, n_rep, edge, chan, n_own, first_own, share, chunk = sizes
     n_all = n_row * n_col * n_rep
     pairs = edge // 2
     row, col, rep = lax.axis_index("row"), lax.axis_index("col"), lax.axis_index("rep")
@@ -234,24 +228,24 @@
             device_id_type=MESH,
         )
 
-    def col_copy(k, src):
+    def col_copy(to, src):
         return pltpu.make_async_remote_copy(
             src_ref=colbuf.at[src],
             dst_ref=colbuf.at[src],
             send_sem=col_send,
             recv_sem=col_recv,
-            device_id={"row": far(k)},
+            device_id={"row": to},
             device_id_type=MESH,
         )
 
-    def cedge_copy(side, d, src):
+    def cedge_copy(side, at, src):
         to = lax.rem(col + (1 if side == 0 else n_col - 1), n_col)
         return pltpu.make_async_remote_copy(
             src_ref=coltail.at[side],
             dst_ref=coledge.at[side, src],
             send_sem=cedge_send,
             recv_sem=cedge_recv,
-            device_id={"row": lax.rem(row + d, n_row), "col": to},
+            device_id={"row": at, "col": to},
             device_id_type=MESH,
         )
 
@@ -277,25 +271,31 @@
 
     part_col = pl.run_scoped(project_col, pltpu.ACC(0)((rank, 256), F32))
     colbuf[row] = part_col.astype(BF16)
-    pl.semaphore_wait(barrier, n_all - 1)
-    loop(0, n_row - 1, lambda k: col_copy(k, row).start())
     turned = rounded(part_col).T
     for side in range(2):
         coltail[side] = pair_row(turned, ends[side])
-    for side in range(2):
-        loop(0, n_row, lambda d: cedge_copy(side, d, row).start())
-
     for copy in inputs[2:4]:
         copy.wait()
     part_row = pl.run_scoped(project_row, pltpu.ACC(1)((rank, 256), F32))
     keep = kept[0, 0].astype(F32)
     rowbuf[col, 0:rank, :] = part_row.astype(BF16)
     rowbuf[col, rank:, :] = jnp.full((16, edge), keep, F32).astype(BF16)
-    loop(1, n_col, lambda d: row_copy(d, col).start())
     turned = rounded(part_row).T
     for side in range(2):
         rowtail[side, 0:1] = pair_row(turned, ends[side])
         rowtail[side, 1:2] = jnp.full((1, 2 * rank), keep, F32)
+    pl.semaphore_wait(barrier, n_all - 1)
+
+    def send_col(k):
+        to = far(k)
+        col_copy(to, row).start()
+        for side in range(2):
+            cedge_copy(side, to, row).start()
+
+    loop(0, n_row - 1, send_col)
+    for side in range(2):
+        cedge_copy(side, row, row).start()
+    loop(1, n_col, lambda d: row_copy(d, col).start())
     for side in range(2):
         loop(0, n_col, lambda d: redge_copy(side, d, col).start())
 
@@ -386,8 +386,8 @@
     shifted = [col_wide[6 + 2 * b : 6 + 2 * b + edge, :].T for b in range(3)]
     first_rows = lax.broadcasted_iota(jnp.int32, (2 * edge - 2 * rank, 2 * edge), 0) < 3
 
-    def operand(b, mask):
-        value = shifted[b] * mask
+    def operand(value, mask):
+        value = value * mask
         blank = jnp.zeros_like(value)
         ones = jnp.where(first_rows, jnp.concatenate([mask, mask], axis=1), 0.0)
         return jnp.concatenate(
@@ -399,8 +399,21 @@
             axis=0,
         ).astype(BF16)
 
-    for b in range(3):
-        wide[b] = operand(b, middle[b])
+    def outer(left, right):
+        return jnp.where(lane < 2, left, jnp.where(lane >= edge - 2, right, 0.0))
+
+    wide[0] = operand(shifted[1], middle[1])
+    wide[1] = operand(outer(shifted[0], shifted[2]), outer(middle[0], middle[2]))
+    lane_wide = lax.broadcasted_iota(jnp.int32, (chan, edge), 1)
+
+    def moved(value, halo, b):
+        halves = []
+        for r in range(2):
+            lanes = slice(r * edge, (r + 1) * edge)
+            turned = pltpu.roll(value[:, lanes], 2 if b == 0 else edge - 2, 1)
+            at_end = lane_wide < 2 if b == 0 else lane_wide >= edge - 2
+            halves.append(jnp.where(at_end, halo[:, lanes], turned))
+        return jnp.concatenate(halves, axis=1)
 
     def scaled(p, count):
         low = (out_t * feat_pairs[pl.ds(p + 1 + r, 1), :] for r in range(count))
@@ -427,12 +440,12 @@
         loss_out[pl.ds(at + 1, 1), :] = loss[:, edge : 2 * edge]
 
     def main(*accs):
-        sums, grads, halo, features_of = accs[0:4], accs[4:6], accs[6], (accs[7:10], accs[10:16])
+        sums, grads, halo, features_of = accs[0:4], accs[4:6], accs[6], (accs[7:9], accs[9:13])
         stage, primed = [0, 0], [False, False]
 
         def halo_item(p, offset, b, mask):
             def push(at):
-                pltpu.matmul_push_rhs(operand(b, mask[b]), at, 1)
+                pltpu.matmul_push_rhs(operand(shifted[b], mask[b]), at, 1)
 
             def go(at):
                 pltpu.matmul_acc_lhs(halo, scaled(p + offset, 1), load_staged_rhs=at)
@@ -441,24 +454,27 @@
 
             return push, go, None, 4
 
-        def feature_item(unit, b, p, offset, acc, memo):
+        def feature_item(unit, kind, p, offset, held, memo):
             def push(at):
-                pltpu.matmul_push_rhs(wide[b], at, unit)
+                pltpu.matmul_push_rhs(wide[kind], at, unit)
 
             def go(at):
-                if offset not in memo:
-                    memo[offset] = scaled(p + offset, 2)
-                pltpu.matmul_acc_lhs(acc, memo[offset], load_staged_rhs=at)
+                if not memo:
+                    memo.append(scaled(p + offset, 2))
+                pltpu.matmul_acc_lhs(held[kind], memo[0], load_staged_rhs=at)
 
             def after():
-                value = pltpu.matmul_pop(acc)
+                value, halo = (pltpu.matmul_pop(acc) for acc in held)
                 for r in range(2):
                     own = value[r * chan : (r + 1) * chan]
-                    hid[slot(offset + r, b, 1, 3), :] = jnp.maximum(own, 0.0).astype(BF16)
-                    if b == 1:
-                        base[slot(offset + r), :] = own + conv_b
-
-            return push, go, after, 8
+                    base[slot(offset + r), :] = own + conv_b
+                    own = jnp.maximum(own, 0.0)
+                    ends_of = jnp.maximum(halo[r * chan : (r + 1) * chan], 0.0)
+                    for b in range(3):
+                        copy_of = own if b == 1 else moved(own, ends_of, b)
+                        hid[slot(offset + r, b, 1, 3), :] = copy_of.astype(BF16)
+
+            return push, go, after if kind == 1 else None, 8
 
         def conv_item(p, offset):
             taps = [a for a in range(3) if inside(p, offset + 1 - a)]
@@ -532,13 +548,9 @@
         def features(p, low, units=(1, 1)):
             items = []
             for half, unit in enumerate(units):
-                memo = {}
-                held = features_of[unit][3 * half * unit : 3 * half * unit + 3]
+                memo, held = [], features_of[unit][2 * half * unit : 2 * half * unit + 2]
                 items.append(
-                    [
-                        feature_item(unit, b, p, low + 2 * half, held[b], memo)
-                        for b in range(3)
-                    ]
+                    [feature_item(unit, k, p, low + 2 * half, held, memo) for k in range(2)]
                 )
             return items
 
@@ -551,10 +563,12 @@
         def group(p, low):
             early, late = features(p, low)
             conv = convs(p, low - 4, low)
+            shared = [turns(0, p, low - 10), turns(1, p, low - 10)]
+            shared[1 if low % 8 == 0 else 0] = []
             run(
                 (
-                    turns(0, p, low - 12) + conv[0:2] + turns(0, p, low - 10) + conv[2:4],
-                    turns(1, p, low - 11) + early + turns(1, p, low - 9) + late,
+                    turns(0, p, low - 12) + conv[0:2] + shared[0] + conv[2:4],
+                    turns(1, p, low - 11) + early + shared[1] + turns(1, p, low - 9) + late,
                 ),
                 [turns(u, p, low - 8 + u)[0] for u in range(2)],
             )
@@ -604,8 +618,8 @@
         *[accumulator(0, chan)] * 4,
         *[accumulator(unit, 3 * chan) for unit in range(2)],
         accumulator(1, chan),
-        *[accumulator(0, 2 * chan)] * 3,
-        *[accumulator(1, 2 * chan)] * 6,
+        *[accumulator(0, 2 * chan)] * 2,
+        *[accumulator(1, 2 * chan)] * 4,
     )
 
     norm = 1.0 / (edge * edge)
@@ -624,25 +638,39 @@
     bias_sum = (bias_acc[:, 0:edge] + bias_acc[:, edge:]).T
     bias_sum = jnp.sum(bias_sum, axis=0, keepdims=True) * norm
 
-    def coded(values, most):
-        most = jnp.maximum(most, 1e-33)
-        return jnp.round(values * (32767.0 / most)).astype(jnp.int32), most / 32767.0
-
     def largest(values):
         return jnp.max(jnp.max(jnp.abs(values), axis=0, keepdims=True), axis=1, keepdims=True)
 
-    def side_row(bias, scale):
-        return jnp.concatenate([bias, jnp.broadcast_to(scale, (1, 128 - chan))], axis=1)
-
-    codes, scale = coded(flat, largest(flat))
+    def exponent(values):
+        return jnp.ceil(jnp.log(jnp.maximum(largest(values), 1e-30)) * LOG2E + 0.01)
+
+    def coded(values, power):
+        return values * (jnp.exp2(-power) * CODES)
+
+    def side_rows(power, bias):
+        bias_power = exponent(bias)
+        high = jnp.round(coded(bias, bias_power))
+        low = (coded(bias, bias_power) - high) * CODES
+        return [
+            jnp.concatenate([high, low], axis=1),
+            jnp.broadcast_to(power, (1, 128)),
+            jnp.broadcast_to(bias_power, (1, 128)),
+        ]
+
+    def packed(values, sides):
+        blank = chunk - values.shape[0] - len(sides)
+        values = jnp.concatenate([values, *sides, jnp.zeros((blank, 128), F32)], axis=0)
+        return jnp.round(values).astype(jnp.int32).astype(jnp.int16)
+
+    power = exponent(flat)
+    codes = coded(flat, power)
+    sides = side_rows(power, bias_sum)
     for index in range(n_own):
-        have = min(max(rows - index * chunk, 0), chunk)
-        values = [codes[index * chunk : index * chunk + have]] if have else []
-        if have < chunk:
-            values.append(jnp.zeros((chunk - have, 128), jnp.int32))
-        values = jnp.concatenate(values, axis=0)
-        part[index] = values.astype(jnp.int16)
-    own_side[...] = side_row(bias_sum, scale)
+        have = min(max(rows - index * share, 0), share)
+        values = [codes[index * share : index * share + have]] if have else []
+        if have < share:
+            values.append(jnp.zeros((share - have, 128), F32))
+        part[index] = packed(jnp.concatenate(values, axis=0), sides)
 
     mine = me - first_own
     owner = (mine >= 0) & (mine < n_own)
@@ -657,75 +685,90 @@
             device_id_type=MESH,
         )
 
+    square_of = n_col * n_rep
+    owner_rows = n_own // square_of
+
     def scatter(d):
-        index = lax.rem(me + d, n_own)
+        level = d // square_of if isinstance(d, int) else lax.div(d, square_of)
+        level = jnp.where(2 * row < n_row, owner_rows - 1 - level, level)
+        index = level * square_of + lax.rem(me + d, square_of)
 
         @pl.when(first_own + index != me)
         def _():
             to = device(first_own + index)
             remote(part.at[index], reduced.at[me], rs_send, rs_recv, to).start()
-            remote(own_side, sides.at[me], side_send, side_recv, to).start()
-
-    def gather(d):
-        to = device(lax.rem(me + d, n_all))
+
+    def give(to):
         remote(full.at[mine], full.at[mine], ag_send, ag_recv, to).start()
-        remote(full_side.at[mine], full_side.at[mine], full_send, full_recv, to).start()
+
+    def around(at):
+        for c in range(n_col - 1, -1, -1):
+            for r in range(n_rep - 1, -1, -1):
+                yield {"row": at, "col": wrapped(col + c, n_col), "rep": wrapped(rep + r, n_rep)}
+
+    def gather(k):
+        for to in around(far(k)):
+            give(to)
 
     loop(0, n_own, scatter)
 
     @pl.when(owner)
     def _():
         reduced[me] = part[mine]
-        sides[me] = own_side[...]
-        await_bytes(sides.at[0 : n_all - 1], side_recv)
         await_bytes(reduced.at[0 : n_all - 1], rs_recv)
 
         def decoded(r):
-            return reduced[r].astype(jnp.int32).astype(F32) * sides[r][:, 127:128]
+            value = reduced[r].astype(jnp.int32).astype(F32)
+            return (
+                value[0:share] * (jnp.exp2(value[share + 1 : share + 2]) / CODES),
+                value[share : share + 1] * (jnp.exp2(value[share + 2 : share + 3]) / CODES),
+            )
 
         if n_all <= 16:
-            own = sum(decoded(r) for r in range(n_all))
-            bias = sum(sides[r] for r in range(n_all))
+            terms = [decoded(r) for r in range(n_all)]
+            own, bias = (sum(x[k] for x in terms) for k in range(2))
         else:
-            own = lax.fori_loop(
-                0, n_all, lambda r, x: x + decoded(r), jnp.zeros((chunk, 128), F32)
+            own, bias = lax.fori_loop(
+                0,
+                n_all,
+                lambda r, x: tuple(a + b for a, b in zip(x, decoded(r))),
+                (jnp.zeros((share, 128), F32), jnp.zeros((1, 128), F32)),
             )
-            bias = lax.fori_loop(0, n_all, lambda r, x: x + sides[r], jnp.zeros((1, 128), F32))
-        codes, scale = coded(own, largest(own))
-        full[mine] = codes.astype(jnp.int16)
-        full_side[mine] = side_row(bias[:, 0:chan], scale)
-        loop(1, n_all, gather)
+        bias = bias[:, 0:chan] + bias[:, chan : 2 * chan] * (1.0 / CODES)
+        power = exponent(own)
+        full[mine] = packed(coded(own, power), side_rows(power, bias))
+        loop(0, n_row - 1, gather)
+        for to in list(around(row))[:-1]:
+            give(to)
         if n_own > 1:
-            await_bytes(full_side.at[0 : n_own - 1], full_recv)
             await_bytes(full.at[0 : n_own - 1], ag_recv)
-            await_bytes(sides.at[0 : n_own - 1], side_send)
             await_bytes(part.at[0 : n_own - 1], rs_send)
 
     @pl.when(jnp.logical_not(owner))
     def _():
-        await_bytes(full_side, full_recv)
         await_bytes(full, ag_recv)
-        await_bytes(sides.at[0:n_own], side_send)
         await_bytes(part, rs_send)
 
     await_features(col_send, row_send, cedge_send, redge_send)
 
     @pl.when(owner)
     def _():
-        await_bytes(sides.at[0 : n_all - 1], full_send)
         await_bytes(reduced.at[0 : n_all - 1], ag_send)
 
 
-def finish(loss, gathered, side, loss_hbm, conv_grad_hbm, bias_hbm, full, conv_grad_out, bias_out, sem):
-    n_all, chunk = gathered.shape[0:2]
+def finish(share, loss, gathered, loss_hbm, conv_grad_hbm, bias_hbm, full, conv_grad_out, bias_out, sem):
+    n_own = gathered.shape[0]
     loss_copy = pltpu.make_async_copy(loss, loss_hbm, sem.at[0])
     loss_copy.start()
 
-    def place(r):
-        value = gathered[r].astype(jnp.int32).astype(F32) * side[r][:, 127:128]
-        full[pl.ds(r * chunk, chunk), :] = value
-
-    loop(0, n_all, place)
+    def decoded(r, low, high, power):
+        value = gathered[r].astype(jnp.int32).astype(F32)
+        return value[low:high] * (jnp.exp2(value[power : power + 1]) / CODES)
+
+    for r in range(min(n_own, pl.cdiv(full.shape[0], share))):
+        high = min(share, full.shape[0] - r * share)
+        full[r * share : r * share + high, :] = decoded(r, 0, high, share + 1)
+
     chan = bias_out.shape[1]
     half = 3 * chan // 2
     rows = 3 * chan + half
@@ -738,7 +781,8 @@
     conv_grad_out[2, 1, 0 : half - chan] = full[low + chan : low + half, 0:chan]
     conv_grad_out[2, 1, half - chan :] = full[low : low + 2 * chan - half, chan : 2 * chan]
     conv_grad_out[2, 2] = full[low + 2 * chan - half : low + half, chan : 2 * chan]
-    bias_out[...] = side[0][:, 0:chan]
+    terms = decoded(0, share, share + 1, share + 2)
+    bias_out[...] = terms[:, 0:chan] + terms[:, chan : 2 * chan] * (1.0 / CODES)
     grad_copy = pltpu.make_async_copy(conv_grad_out, conv_grad_hbm, sem.at[1])
     bias_copy = pltpu.make_async_copy(bias_out, bias_hbm, sem.at[2])
     grad_copy.start()
@@ -771,7 +815,8 @@
         inner = n_row // 2 if n_row >= 4 else n_row
         n_own = inner * n_col * n_rep
         first_own = (n_row - inner) // 2 * n_col * n_rep
-        chunk = 8 * pl.cdiv(used, 8 * n_own)
+        share = pl.cdiv(used, n_own)
+        chunk = 8 * pl.cdiv(share + 3, 8)
 
         def window(width, count):
             return window_of(proj_row.shape[0], width, 0, count)[1]
@@ -781,15 +826,14 @@
         hbm = pl.BlockSpec(memory_space=pltpu.HBM)
         results = pl.pallas_call(
             functools.partial(
-                kernel, (n_row, n_col, n_rep, edge, chan, n_own, first_own, chunk)
+                kernel, (n_row, n_col, n_rep, edge, chan, n_own, first_own, share, chunk)
             ),
             out_shape=(
                 pltpu.VMEM((edge, edge), F32),
                 pltpu.VMEM((n_own, chunk, 128), jnp.int16),
-                pltpu.VMEM((n_own, 1, 128), F32),
             ),
             in_specs=[hbm] * 9 + [pl.BlockSpec(memory_space=pltpu.SMEM)],
-            out_specs=(vmem,) * 3,
+            out_specs=(vmem,) * 2,
             scratch_shapes=[
                 pltpu.VMEM(emb_row.shape, BF16),
                 pltpu.VMEM(emb_col.shape[::-1], BF16),
@@ -810,7 +854,7 @@
                 pltpu.VMEM((edge + 16, rank), F32),
                 pltpu.VMEM((pairs + 8, 2 * rank), F32),
                 pltpu.VMEM((256, 256), BF16),
-                pltpu.VMEM((3, 2 * edge, 2 * edge), BF16),
+                pltpu.VMEM((2, 2 * edge, 2 * edge), BF16),
                 pltpu.VMEM((3 * chan, 4 * chan), BF16),
                 pltpu.VMEM((chan, edge, edge), BF16),
                 pltpu.VMEM((pairs * chan, 2 * edge), BF16),
@@ -822,9 +866,7 @@
                 pltpu.VMEM((chan, 2 * edge), F32),
                 pltpu.VMEM((n_own, chunk, 128), jnp.int16),
                 pltpu.VMEM((n_all, chunk, 128), jnp.int16),
-                pltpu.VMEM((1, 128), F32),
-                pltpu.VMEM((n_all, 1, 128), F32),
-                *[pltpu.SemaphoreType.DMA] * 17,
+                *[pltpu.SemaphoreType.DMA] * 13,
             ],
             compiler_params=pltpu.CompilerParams(collective_id=0, has_side_effects=True),
             name="pair_step",
@@ -841,16 +883,16 @@
             kept_tiles,
         )
         loss, grads, bias = pl.pallas_call(
-            finish,
+            functools.partial(finish, share),
             out_shape=(
                 jax.ShapeDtypeStruct((edge, edge), F32),
                 jax.ShapeDtypeStruct((3, 3, chan, chan), F32),
                 jax.ShapeDtypeStruct((1, chan), F32),
             ),
-            in_specs=[vmem] * 3,
+            in_specs=[vmem] * 2,
             out_specs=(hbm,) * 3,
             scratch_shapes=[
-                pltpu.VMEM((n_own * chunk, 128), F32),
+                pltpu.VMEM((used, 128), F32),
                 pltpu.VMEM((3, 3, chan, chan), F32),
                 pltpu.VMEM((1, chan), F32),
                 dma((3,)),

time: 28.3 us -> 27.9 us (0.986)
  Pallas kernels: 26.8 us -> 26.5 us
where the time goes in v5:
time: 27.9 us; the launch traced here: 27.8 us
  Pallas kernels  26.5 us (95%)
  between operations  1.29 us (5%)
    pallas_call x1, Pallas kernels, per_device(): pl.pallas_call(functools.partial(kernel, (n_row, n_col, n_rep, edge, chan...  25.6 us
    pallas_call x1, Pallas kernels, per_device(): pl.pallas_call(functools.partial(finish, share), out_shape=(jax.ShapeDtyp...  0.87 us

profile of v5, /device:TPU:0, one launch (start us, length us, event | category | flops | bytes accessed | tf_op | source)
XLA Modules:
  0.0 27.8 jit_solution(8922742966394450902)
XLA Ops:
  1.3 25.6 %pair_step.1 = (f32[128,128]{1,0:T(8,128)S(1)}, s16[8,40,128]{2,1,0:T(8,128)(2,1)S(1)}) custom-call(bf16[128,640]{1,0:T(8,128)(2,1)} %emb_row_hbm.1, bf16[320,128]{1,0:T(8,128)(2,1)} %bitcast.8, bf16[64,1280]{1,0:T(8,128)(2,1)} %bitcast.6, bf16[64,1280]{1,0:T(8,128)(2,1)} %bitcast.7, bf16[64,64]{1,0:T(8,128)(2,1)} %pair_out_hbm.1, f32[1,64]{1,0:T(1,128)} %bitcast.9, ...), custom_call_target="tpu_custom_call" | custom-call | tf_op jit(solution)/shard_map/pair_step/pallas_call | solution.py:827
  26.9 0.9 %finish.1 = (f32[128,128]{1,0:T(8,128)}, f32[3,3,64,64]{3,2,1,0:T(8,128)}, f32[1,64]{1,0:T(1,128)}) custom-call(f32[128,128]{1,0:T(8,128)S(1)} %get-tuple-element.8.loss, s16[8,40,128]{2,1,0:T(8,128)(2,1)S(1)} %get-tuple-element.9.gathered), custom_call_target="tpu_custom_call" | custom-call | tf_op jit(solution)/shard_map/finish/pallas_call | solution.py:885

commit v6 on v5

--- a/solution.py
+++ b/solution.py
@@ -440,12 +440,15 @@
         loss_out[pl.ds(at + 1, 1), :] = loss[:, edge : 2 * edge]
 
     def main(*accs):
-        sums, grads, halo, features_of = accs[0:4], accs[4:6], accs[6], (accs[7:9], accs[9:13])
+        sums, grads, halos = accs[0:4], accs[4:6], accs[6:8]
+        features_of = (accs[8:10], accs[10:14])
         stage, primed = [0, 0], [False, False]
 
-        def halo_item(p, offset, b, mask):
+        def halo_item(unit, p, offset, b, mask):
+            halo = halos[unit]
+
             def push(at):
-                pltpu.matmul_push_rhs(operand(shifted[b], mask[b]), at, 1)
+                pltpu.matmul_push_rhs(operand(shifted[b], mask[b]), at, unit)
 
             def go(at):
                 pltpu.matmul_acc_lhs(halo, scaled(p + offset, 1), load_staged_rhs=at)
@@ -573,10 +576,11 @@
                 [turns(u, p, low - 8 + u)[0] for u in range(2)],
             )
 
-        early, late = features(0, 0, (1, 0))
+        early, late = features(0, 0)
         first = convs(0, -1, 4)
         second = features(0, 4)
-        run((late, [halo_item(0, -1, b, top) for b in range(3)] + early), (first[0], second[0][0]))
+        tops = [halo_item(0, 0, -1, b, top) for b in range(3)]
+        run((tops, early + late), (first[0], second[0][0]))
         third, fourth = convs(0, 4, 8), features(0, 8)
         run((first, second[0] + second[1]), (third[0], fourth[0][0]))
         fifth, sixth = convs(0, 8, 12), features(0, 12)
@@ -601,7 +605,7 @@
             (
                 turns(0, pairs, -12) + last[0:2] + turns(0, pairs, -10) + last[2:4],
                 turns(1, pairs, -11)
-                + [halo_item(pairs, 0, b, bottom) for b in range(3)]
+                + [halo_item(1, pairs, 0, b, bottom) for b in range(3)]
                 + turns(1, pairs, -9, -8, -7),
             ),
             (last[4], turns(1, pairs, -6)[0]),
@@ -617,7 +621,7 @@
         main,
         *[accumulator(0, chan)] * 4,
         *[accumulator(unit, 3 * chan) for unit in range(2)],
-        accumulator(1, chan),
+        *[accumulator(unit, chan) for unit in range(2)],
         *[accumulator(0, 2 * chan)] * 2,
         *[accumulator(1, 2 * chan)] * 4,
     )

time: 27.9 us -> 27.9 us (level)
  no operation moved by 1% of the time
where the time goes in v6:
time: 27.9 us; the launch traced here: 27.7 us
  Pallas kernels  26.4 us (95%)
  between operations  1.29 us (5%)
    pallas_call x1, Pallas kernels, per_device(): pl.pallas_call(functools.partial(kernel, (n_row, n_col, n_rep, edge, chan...  25.5 us
    pallas_call x1, Pallas kernels, per_device(): pl.pallas_call(functools.partial(finish, share), out_shape=(jax.ShapeDtyp...  0.87 us

profile of v6, /device:TPU:0, one launch (start us, length us, event | category | flops | bytes accessed | tf_op | source)
XLA Modules:
  0.0 27.7 jit_solution(2585778352996003017)
XLA Ops:
  1.3 25.5 %pair_step.1 = (f32[128,128]{1,0:T(8,128)S(1)}, s16[8,40,128]{2,1,0:T(8,128)(2,1)S(1)}) custom-call(bf16[128,640]{1,0:T(8,128)(2,1)} %emb_row_hbm.1, bf16[320,128]{1,0:T(8,128)(2,1)} %bitcast.8, bf16[64,1280]{1,0:T(8,128)(2,1)} %bitcast.6, bf16[64,1280]{1,0:T(8,128)(2,1)} %bitcast.7, bf16[64,64]{1,0:T(8,128)(2,1)} %pair_out_hbm.1, f32[1,64]{1,0:T(1,128)} %bitcast.9, ...), custom_call_target="tpu_custom_call" | custom-call | tf_op jit(solution)/shard_map/pair_step/pallas_call | solution.py:831
  26.8 0.9 %finish.1 = (f32[128,128]{1,0:T(8,128)}, f32[3,3,64,64]{3,2,1,0:T(8,128)}, f32[1,64]{1,0:T(1,128)}) custom-call(f32[128,128]{1,0:T(8,128)S(1)} %get-tuple-element.8.loss, s16[8,40,128]{2,1,0:T(8,128)(2,1)S(1)} %get-tuple-element.9.gathered), custom_call_target="tpu_custom_call" | custom-call | tf_op jit(solution)/shard_map/finish/pallas_call | solution.py:889

commit v7 on v6

--- a/solution.py
+++ b/solution.py
@@ -764,6 +764,10 @@
     n_own = gathered.shape[0]
     loss_copy = pltpu.make_async_copy(loss, loss_hbm, sem.at[0])
     loss_copy.start()
+    grad_copies = [
+        pltpu.make_async_copy(conv_grad_out.at[a], conv_grad_hbm.at[a], sem.at[2 + a])
+        for a in range(3)
+    ]
 
     def decoded(r, low, high, power):
         value = gathered[r].astype(jnp.int32).astype(F32)
@@ -779,7 +783,11 @@
     for b in range(3):
         low = b * chan
         conv_grad_out[1, b] = full[low : low + chan, 0:chan]
+    grad_copies[1].start()
+    for b in range(3):
+        low = b * chan
         conv_grad_out[0, b] = full[low : low + chan, chan : 2 * chan]
+    grad_copies[0].start()
     low = 3 * chan
     conv_grad_out[2, 0] = full[low : low + chan, 0:chan]
     conv_grad_out[2, 1, 0 : half - chan] = full[low + chan : low + half, 0:chan]
@@ -787,12 +795,12 @@
     conv_grad_out[2, 2] = full[low + 2 * chan - half : low + half, chan : 2 * chan]
     terms = decoded(0, share, share + 1, share + 2)
     bias_out[...] = terms[:, 0:chan] + terms[:, chan : 2 * chan] * (1.0 / CODES)
-    grad_copy = pltpu.make_async_copy(conv_grad_out, conv_grad_hbm, sem.at[1])
-    bias_copy = pltpu.make_async_copy(bias_out, bias_hbm, sem.at[2])
-    grad_copy.start()
+    bias_copy = pltpu.make_async_copy(bias_out, bias_hbm, sem.at[1])
+    grad_copies[2].start()
     bias_copy.start()
     loss_copy.wait()
-    grad_copy.wait()
+    for copy in grad_copies:
+        copy.wait()
     bias_copy.wait()
 
 
@@ -899,7 +907,7 @@
                 pltpu.VMEM((used, 128), F32),
                 pltpu.VMEM((3, 3, chan, chan), F32),
                 pltpu.VMEM((1, chan), F32),
-                dma((3,)),
+                dma((5,)),
             ],
             name="finish",
         )(

time: 27.9 us -> 27.8 us (level)
  no operation moved by 1% of the time
where the time goes in v7:
time: 27.8 us; the launch traced here: 27.7 us
  Pallas kernels  26.4 us (95%)
  between operations  1.29 us (5%)
    pallas_call x1, Pallas kernels, per_device(): pl.pallas_call(functools.partial(kernel, (n_row, n_col, n_rep, edge, chan...  25.5 us
    pallas_call x1, Pallas kernels, per_device(): pl.pallas_call(functools.partial(finish, share), out_shape=(jax.ShapeDtyp...  0.83 us

profile of v7, /device:TPU:0, one launch (start us, length us, event | category | flops | bytes accessed | tf_op | source)
XLA Modules:
  0.0 27.7 jit_solution(3688509714262642805)
XLA Ops:
  1.3 25.5 %pair_step.1 = (f32[128,128]{1,0:T(8,128)S(1)}, s16[8,40,128]{2,1,0:T(8,128)(2,1)S(1)}) custom-call(bf16[128,640]{1,0:T(8,128)(2,1)} %emb_row_hbm.1, bf16[320,128]{1,0:T(8,128)(2,1)} %bitcast.8, bf16[64,1280]{1,0:T(8,128)(2,1)} %bitcast.6, bf16[64,1280]{1,0:T(8,128)(2,1)} %bitcast.7, bf16[64,64]{1,0:T(8,128)(2,1)} %pair_out_hbm.1, f32[1,64]{1,0:T(1,128)} %bitcast.9, ...), custom_call_target="tpu_custom_call" | custom-call | tf_op jit(solution)/shard_map/pair_step/pallas_call | solution.py:839
  26.8 0.8 %finish.1 = (f32[128,128]{1,0:T(8,128)}, f32[3,3,64,64]{3,2,1,0:T(8,128)}, f32[1,64]{1,0:T(1,128)}) custom-call(f32[128,128]{1,0:T(8,128)S(1)} %get-tuple-element.8.loss, s16[8,40,128]{2,1,0:T(8,128)(2,1)S(1)} %get-tuple-element.9.gathered), custom_call_target="tpu_custom_call" | custom-call | tf_op jit(solution)/shard_map/finish/pallas_call | solution.py:897
